TPU v7x, 128 devices: a whole 4x4x4 slice. The times are simulated.
128 devices in a mesh: section: 16 (over z_lo, x, core), tensor: 8 (over z_hi, y).
Axes of the slice: x: 4, y: 4, z: 4 (z_hi: 2, z_lo: 2; z = z_hi * 2 + z_lo), core: 2. Of those that a mesh axis runs over, the one named last changes fastest.
Arguments:
- matching: int32 [16], replicated, may hold values from 0 to 15, each once
- lengths: int32 [32], replicated, may hold values from 2 to 255
- queries: bfloat16 [16, 32, 8192], P('section', None, 'tensor'), may hold values from -200 to 200
- kv_cache: bfloat16 [16, 32, 256, 2048], P('section', None, None, 'tensor'), may hold values from -6 to 6
- incoming_key_value: bfloat16 [16, 32, 2048], P('section', None, 'tensor'), may hold values from -6 to 6
- residual: bfloat16 [16, 32, 8192], P('section', None, 'tensor'), may hold values from -6 to 6
- out_weight: bfloat16 [16, 8192, 8192], P('section', 'tensor'), may hold values from -0.09375 to 0.09375
- norm_gain: bfloat16 [16, 8192], P('section', 'tensor'), may hold values from 0.5 to 1.5
Outputs:
- cache_out: bfloat16 [16, 32, 256, 2048], P('section', None, None, 'tensor')
- stream_out: bfloat16 [16, 32, 8192], P('section', None, 'tensor')
- normed_out: bfloat16 [16, 32, 8192], P('section', None, 'tensor')
All inputs are finite; a program needn't handle non-finite values.
Results may differ from a plain program's by a relative error of at most 0.0042.
Values may be sent and summed in bfloat16 or wider, within the bound.
A program may use at most 128 MiB of HBM per device.

v0:
```python
import math

import jax
import jax.numpy as jnp
from jax import lax
from jax.sharding import PartitionSpec as P

D = 8192
HEAD_SIZE = 128


def in_blocks(array, dim, count):
    shape = array.shape
    pieces = array.reshape(*shape[:dim], count, shape[dim] // count, *shape[dim + 1 :])
    return jnp.moveaxis(pieces, dim, 0)


def sum_at_owner(array, axis, dim):
    pieces = in_blocks(array, dim, lax.axis_size(axis))
    arrived = lax.all_to_all(pieces, axis, split_axis=0, concat_axis=0, tiled=True)
    return arrived.sum(axis=0)


def from_everyone(array, axis):
    count = lax.axis_size(axis)
    return lax.all_to_all(
        jnp.broadcast_to(array[None], (count, *array.shape)), axis, 0, 0, tiled=True
    )


def of_everyone(array, axis):
    everything = from_everyone(array, axis)
    return jnp.sum(everything, axis=0)


def fold_rows(member, groups):
    return member.reshape((groups, member.shape[1] // groups) + member.shape[2:])


def attend(lengths, query_vectors, cache_rows, fresh_rows):
    seq_rows, ctx_len, kv_width = cache_rows.shape
    kv_heads = kv_width // (2 * HEAD_SIZE)
    places = lax.broadcasted_iota(jnp.int32, (seq_rows, ctx_len), 1)
    written = places == lengths[:, None]
    updated_cache = jnp.where(written[:, :, None], fresh_rows[:, None, :], cache_rows)
    heads_separated = updated_cache.reshape(seq_rows, ctx_len, kv_heads, 2, HEAD_SIZE)
    key_rows = heads_separated[:, :, :, 0]
    value_rows = heads_separated[:, :, :, 1]
    grouped_queries = query_vectors.reshape(seq_rows, kv_heads, -1, HEAD_SIZE)
    scores = jnp.einsum(
        "bgrd,bsgd->bgrs", grouped_queries, key_rows, preferred_element_type=jnp.float32
    ) / math.sqrt(HEAD_SIZE)
    visible = places <= lengths[:, None]
    scores = jnp.where(visible[:, None, None, :], scores, -1e30)
    weights = jax.nn.softmax(scores, axis=-1).astype(jnp.bfloat16)
    attended = jnp.einsum(
        "bgrs,bsgd->bgrd", weights, value_rows, preferred_element_type=jnp.float32
    )
    return (updated_cache, attended.astype(jnp.bfloat16).reshape(seq_rows, -1))


def decode_layer(lengths, queries, kv_cache, incoming_key_value, residual, out_weight, norm_gain):
    updated_cache, attended = attend(lengths, queries[0], kv_cache[0], incoming_key_value[0])
    partial_value = jnp.dot(attended, out_weight[0], preferred_element_type=jnp.float32)
    own_res = residual[0].astype(jnp.float32)
    stream = own_res + sum_at_owner(partial_value, "tensor", 1)
    squares = of_everyone(jnp.sum(stream * stream, axis=-1, keepdims=True), "tensor")
    normed = stream * lax.rsqrt(squares / D + 1e-05) * norm_gain[0].astype(jnp.float32)
    return (
        updated_cache[None],
        stream.astype(jnp.bfloat16)[None],
        normed.astype(jnp.bfloat16)[None],
    )


def move_results(matching, updated_cache, stream, normed):
    groups = lax.axis_size("section")
    spread = (
        lax.all_to_all(
            fold_rows(updated_cache, groups), "section", split_axis=0, concat_axis=0, tiled=True
        ),
        lax.all_to_all(
            fold_rows(stream, groups), "section", split_axis=0, concat_axis=0, tiled=True
        ),
        lax.all_to_all(
            fold_rows(normed, groups), "section", split_axis=0, concat_axis=0, tiled=True
        ),
    )
    landed = (
        lax.all_to_all(
            jnp.take(spread[0], matching, axis=0),
            "section",
            split_axis=0,
            concat_axis=0,
            tiled=True,
        ),
        lax.all_to_all(
            jnp.take(spread[1], matching, axis=0),
            "section",
            split_axis=0,
            concat_axis=0,
            tiled=True,
        ),
        lax.all_to_all(
            jnp.take(spread[2], matching, axis=0),
            "section",
            split_axis=0,
            concat_axis=0,
            tiled=True,
        ),
    )
    return (
        landed[0].reshape(updated_cache.shape),
        landed[1].reshape(stream.shape),
        landed[2].reshape(normed.shape),
    )


def on_device(
    matching, lengths, queries, kv_cache, incoming_key_value, residual, out_weight, norm_gain
):
    updated_cache, stream, normed = decode_layer(
        lengths, queries, kv_cache, incoming_key_value, residual, out_weight, norm_gain
    )
    updated_cache, stream, normed = move_results(matching, updated_cache, stream, normed)
    return (updated_cache, stream, normed)


def solution(mesh):
    return jax.shard_map(
        on_device,
        mesh=mesh,
        in_specs=(
            P(),
            P(),
            P("section", None, "tensor"),
            P("section", None, None, "tensor"),
            P("section", None, "tensor"),
            P("section", None, "tensor"),
            P("section", "tensor", None),
            P("section", "tensor"),
        ),
        out_specs=(
            P("section", None, None, "tensor"),
            P("section", None, "tensor"),
            P("section", None, "tensor"),
        ),
        check_vma=False,
    )
```

profile of v0, /device:TPU:1, one launch (start us, length us, event | category | flops | bytes accessed | tf_op | source)
XLA Modules:
  0.0 263.2 jit_solution(2622778364904964400)
XLA Ops:
  1.4 6.4 %copy.18 = bf16[1,32,256,256]{2,3,1,0:T(8,128)(2,1)} copy(bf16[1,32,256,256]{3,2,1,0:T(8,128)(2,1)} %param.13) | data formatting | bytes 8388608 | tf_op args[3]
  7.8 6.4 %copy.19 = bf16[32,256,1,2,128]{4,1,0,3,2:T(8,128)(2,1)} copy(bf16[32,256,1,2,128]{1,4,3,0,2:T(8,128)(2,1)} %bitcast.43) | data formatting | bytes 8388608 | tf_op jit(solution)/shard_map/squeeze | solution.py:63
  14.3 3.6 %broadcast_select_fusion.1 = bf16[32,256,1,2,128]{4,1,0,3,2:T(8,128)(2,1)S(1)} fusion(bf16[32,256,1,2,128]{4,1,0,3,2:T(8,128)(2,1)} %copy.19, pred[32,256]{1,0:T(8,128)(4,1)S(1)} %get-tuple-element.9, bf16[32,2,128]{2,0,1:T(8,128)(2,1)S(1)} %copy.17), kind=kLoop, calls=%fused_computation.5 | loop fusion | flops 2097152 | bytes 8413184 | tf_op jit(solution)/shard_map/jit(_where)/select_n | solution.py:45
  17.9 2.0 copy-done
  20.8 2.2 fusion.8
  23.0 22.4 %copy.21 = bf16[8192,1024]{1,0:T(8,128)(2,1)} copy(bf16[8192,1024]{0,1:T(8,128)(2,1)} %bitcast.41) | data formatting | bytes 33554432 | tf_op jit(solution)/shard_map/dot_general | solution.py:64
  45.4 10.8 %convolution_bitcast_fusion = f32[8,32,1024]{2,1,0:T(8,128)S(1)} fusion(bf16[32,1024,1]{1,0,2:T(8,128)(2,1)S(1)} %reshape.201, bf16[8,1024,1024]{2,1,0:T(8,128)(2,1)} %bitcast.40), kind=kOutput, calls=%fused_computation.11 | convolution fusion | flops 536870912 | bytes 17891328 | tf_op jit(solution)/shard_map/dot_general | solution.py:64
  56.2 24.4 %all_to_all.40 = f32[8,32,1024]{2,1,0:T(8,128)S(1)} all-to-all(f32[8,32,1024]{2,1,0:T(8,128)S(1)} %convolution_bitcast_fusion), channel_id=1, replica_groups=mesh['section'=16,'tensor'=8] {'tensor'}, dimensions={0} | all-to-all | bytes 2097152 | tf_op jit(solution)/shard_map/all_to_all | solution.py:20
  81.4 3.3 %all-to-all-start.5 = ((f32[8,32,1]{1,2,0:T(1,128)}), f32[8,32,1]{1,2,0:T(1,128)S(1)}, u32[]{:S(2)}, u32[]{:S(2)}) async-start(f32[8,32,1]{1,2,0:T(1,128)} %broadcast_in_dim.80), calls=%async_computation.5 | async-start | bytes 8192 | tf_op jit(solution)/shard_map/all_to_all | solution.py:26
  85.0 6.1 %all-to-all-done.5 = f32[8,32,1]{1,2,0:T(1,128)S(1)} async-done(((f32[8,32,1]{1,2,0:T(1,128)}), f32[8,32,1]{1,2,0:T(1,128)S(1)}, u32[]{:S(2)}, u32[]{:S(2)}) %all-to-all-start.5) | async-done | bytes 1056 | tf_op jit(solution)/shard_map/all_to_all | solution.py:26
  92.0 7.8 %all-to-all-start.3 = ((bf16[16,2,1024]{2,1,0:T(2,128)(2,1)}), bf16[16,2,1024]{2,1,0:T(2,128)(2,1)S(1)}, u32[]{:S(2)}, u32[]{:S(2)}) async-start(bf16[16,2,1024]{2,1,0:T(2,128)(2,1)} %get-tuple-element.5), calls=%async_computation.3 | async-start | bytes 131072 | tf_op jit(solution)/shard_map/all_to_all | solution.py:82
  99.9 5.7 %all-to-all-done.3 = bf16[16,2,1024]{2,1,0:T(2,128)(2,1)S(1)} async-done(((bf16[16,2,1024]{2,1,0:T(2,128)(2,1)}), bf16[16,2,1024]{2,1,0:T(2,128)(2,1)S(1)}, u32[]{:S(2)}, u32[]{:S(2)}) %all-to-all-start.3) | async-done | bytes 65568 | tf_op jit(solution)/shard_map/all_to_all | solution.py:82
  105.6 3.7 %all-to-all-start.6 = ((bf16[16,2,1024]{2,1,0:T(2,128)(2,1)}), bf16[16,2,1024]{2,1,0:T(2,128)(2,1)S(1)}, u32[]{:S(2)}, u32[]{:S(2)}) async-start(bf16[16,2,1024]{2,1,0:T(2,128)(2,1)} %get-tuple-element.4), calls=%async_computation.6 | async-start | bytes 131072 | tf_op jit(solution)/shard_map/all_to_all | solution.py:85
  109.3 5.2 %broadcast_select_fusion.2 = bf16[16,2,256,256]{3,2,1,0:T(8,128)(2,1)} fusion(bf16[16,2,256,256]{3,2,1,0:T(8,128)(2,1)} %bitcast.42, pred[16,2,256]{2,1,0:T(4,128)(4,1)S(1)} %iota_compare_fusion.2, bf16[16,2,256]{2,1,0:T(2,128)(2,1)S(1)} %broadcast_in_dim.71), kind=kLoop, calls=%fused_computation.6 | loop fusion | flops 2097152 | bytes 8413184 | tf_op jit(solution)/shard_map/jit(_where)/select_n | solution.py:45
  115.2 5.3 %all-to-all-start = ((bf16[16,2,256,256]{3,2,1,0:T(8,128)(2,1)}), bf16[16,2,256,256]{3,2,1,0:T(8,128)(2,1)}, u32[]{:S(2)}, u32[]{:S(2)}) async-start(bf16[16,2,256,256]{3,2,1,0:T(8,128)(2,1)} %broadcast_select_fusion.2), calls=%async_computation | async-start | bytes 8388608 | tf_op jit(solution)/shard_map/all_to_all | solution.py:79
  122.7 53.7 %all-to-all-done = bf16[16,2,256,256]{3,2,1,0:T(8,128)(2,1)} async-done(((bf16[16,2,256,256]{3,2,1,0:T(8,128)(2,1)}), bf16[16,2,256,256]{3,2,1,0:T(8,128)(2,1)}, u32[]{:S(2)}, u32[]{:S(2)}) %all-to-all-start) | async-done | bytes 4194336 | tf_op jit(solution)/shard_map/all_to_all | solution.py:79
  176.4 5.1 %all-to-all-start.4 = ((bf16[16,2,1024]{2,1,0:T(2,128)(2,1)}), bf16[16,2,1024]{2,1,0:T(2,128)(2,1)S(1)}, u32[]{:S(2)}, u32[]{:S(2)}) async-start(bf16[16,2,1024]{2,1,0:T(2,128)(2,1)} %get-tuple-element.7), calls=%async_computation.4 | async-start | bytes 131072 | tf_op jit(solution)/shard_map/all_to_all | solution.py:97
  181.5 5.0 %gather_fusion = bf16[16,2,256,256]{3,2,1,0:T(8,128)(2,1)} fusion(bf16[16,2,256,256]{3,2,1,0:T(8,128)(2,1)} %all-to-all-done, s32[1024]{0:T(1024)S(1)} %pad_clamp_fusion), kind=kCustom, calls=%fused_computation.2 | custom fusion | bytes 8388672 | tf_op jit(solution)/shard_map/jit(_take)/gather | solution.py:91
  187.3 4.9 %all-to-all-start.7 = ((bf16[16,2,1024]{2,1,0:T(2,128)(2,1)}), bf16[16,2,1024]{2,1,0:T(2,128)(2,1)S(1)}, u32[]{:S(2)}, u32[]{:S(2)}) async-start(bf16[16,2,1024]{2,1,0:T(2,128)(2,1)} %get-tuple-element.6), calls=%async_computation.7 | async-start | bytes 131072 | tf_op jit(solution)/shard_map/all_to_all | solution.py:104
  192.3 4.7 %broadcast_select_fusion = bf16[16,2,256,256]{3,2,1,0:T(8,128)(2,1)} fusion(bf16[16,2,256,256]{3,2,1,0:T(8,128)(2,1)} %gather_fusion, pred[16]{0:T(512)(128)(4,1)S(1)} %compare_and_fusion), kind=kLoop, calls=%fused_computation.4 | loop fusion | flops 2097152 | bytes 8388624 | tf_op jit(solution)/shard_map/jit(_take)/select_n | solution.py:91
  196.9 1.2 all-to-all-done.7
  198.1 4.7 %all-to-all-start.1 = ((bf16[16,2,256,256]{3,2,1,0:T(8,128)(2,1)}), bf16[16,2,256,256]{3,2,1,0:T(8,128)(2,1)}, u32[]{:S(2)}, u32[]{:S(2)}) async-start(bf16[16,2,256,256]{3,2,1,0:T(8,128)(2,1)} %broadcast_select_fusion), calls=%async_computation.1 | async-start | bytes 8388608 | tf_op jit(solution)/shard_map/all_to_all | solution.py:90
  204.1 54.5 %all-to-all-done.1 = bf16[16,2,256,256]{3,2,1,0:T(8,128)(2,1)} async-done(((bf16[16,2,256,256]{3,2,1,0:T(8,128)(2,1)}), bf16[16,2,256,256]{3,2,1,0:T(8,128)(2,1)}, u32[]{:S(2)}, u32[]{:S(2)}) %all-to-all-start.1) | async-done | bytes 4194336 | tf_op jit(solution)/shard_map/all_to_all | solution.py:90
  258.5 4.6 %copy.24 = bf16[1,32,256,256]{3,2,1,0:T(8,128)(2,1)} copy(bf16[1,32,256,256]{3,2,1,0:T(8,128)(2,1)} %bitcast.1) | data formatting | bytes 8388608
  (43 shorter events, 8.8 us)
Async XLA Ops:
  7.8 6.4 %copy-start.3 = (bf16[1,32,256]{2,1,0:T(8,128)(2,1)S(1)}, bf16[1,32,256]{2,1,0:T(8,128)(2,1)}, u32[]{:S(2)}) copy-start(bf16[1,32,256]{2,1,0:T(8,128)(2,1)} %param.14) | copy-start | bytes 49156
  7.8 6.4 %copy-start.2 = (bf16[1,32,1024]{2,1,0:T(8,128)(2,1)S(1)}, bf16[1,32,1024]{2,1,0:T(8,128)(2,1)}, u32[]{:S(2)}) copy-start(bf16[1,32,1024]{2,1,0:T(8,128)(2,1)} %param.12) | copy-start | bytes 196612
  17.9 2.0 copy-start
  45.4 35.3 %copy-start.1 = (bf16[1,32,1024]{2,1,0:T(8,128)(2,1)S(1)}, bf16[1,32,1024]{2,1,0:T(8,128)(2,1)}, u32[]{:S(2)}) copy-start(bf16[1,32,1024]{2,1,0:T(8,128)(2,1)} %param.15) | copy-start | bytes 196612
  45.4 39.4 %copy-start.5 = (s32[32]{0:T(128)S(1)}, s32[32]{0:T(128)}, u32[]{:S(2)}) copy-start(s32[32]{0:T(128)} %param.11) | copy-start | bytes 388
  45.4 39.5 %copy-start.4 = (bf16[1,1024]{1,0:T(2,128)(2,1)S(1)}, bf16[1,1024]{1,0:T(2,128)(2,1)}, u32[]{:S(2)}) copy-start(bf16[1,1024]{1,0:T(2,128)(2,1)} %param.17) | copy-start | bytes 6148
  81.4 9.7 %all-to-all-start.5 = ((f32[8,32,1]{1,2,0:T(1,128)}), f32[8,32,1]{1,2,0:T(1,128)S(1)}, u32[]{:S(2)}, u32[]{:S(2)}) async-start(f32[8,32,1]{1,2,0:T(1,128)} %broadcast_in_dim.80), calls=%async_computation.5 | async-start | bytes 8192 | tf_op jit(solution)/shard_map/all_to_all | solution.py:26
  92.0 13.6 %all-to-all-start.3 = ((bf16[16,2,1024]{2,1,0:T(2,128)(2,1)}), bf16[16,2,1024]{2,1,0:T(2,128)(2,1)S(1)}, u32[]{:S(2)}, u32[]{:S(2)}) async-start(bf16[16,2,1024]{2,1,0:T(2,128)(2,1)} %get-tuple-element.5), calls=%async_computation.3 | async-start | bytes 131072 | tf_op jit(solution)/shard_map/all_to_all | solution.py:82
  105.6 9.6 %all-to-all-start.6 = ((bf16[16,2,1024]{2,1,0:T(2,128)(2,1)}), bf16[16,2,1024]{2,1,0:T(2,128)(2,1)S(1)}, u32[]{:S(2)}, u32[]{:S(2)}) async-start(bf16[16,2,1024]{2,1,0:T(2,128)(2,1)} %get-tuple-element.4), calls=%async_computation.6 | async-start | bytes 131072 | tf_op jit(solution)/shard_map/all_to_all | solution.py:85
  114.5 5.9 %copy-start.6 = (s32[16]{0:T(128)S(1)}, s32[16]{0:T(128)}, u32[]{:S(2)}) copy-start(s32[16]{0:T(128)} %param.10) | copy-start | bytes 196
  115.2 61.2 %all-to-all-start = ((bf16[16,2,256,256]{3,2,1,0:T(8,128)(2,1)}), bf16[16,2,256,256]{3,2,1,0:T(8,128)(2,1)}, u32[]{:S(2)}, u32[]{:S(2)}) async-start(bf16[16,2,256,256]{3,2,1,0:T(8,128)(2,1)} %broadcast_select_fusion.2), calls=%async_computation | async-start | bytes 8388608 | tf_op jit(solution)/shard_map/all_to_all | solution.py:79
  176.4 10.9 %all-to-all-start.4 = ((bf16[16,2,1024]{2,1,0:T(2,128)(2,1)}), bf16[16,2,1024]{2,1,0:T(2,128)(2,1)S(1)}, u32[]{:S(2)}, u32[]{:S(2)}) async-start(bf16[16,2,1024]{2,1,0:T(2,128)(2,1)} %get-tuple-element.7), calls=%async_computation.4 | async-start | bytes 131072 | tf_op jit(solution)/shard_map/all_to_all | solution.py:97
  187.3 10.7 %all-to-all-start.7 = ((bf16[16,2,1024]{2,1,0:T(2,128)(2,1)}), bf16[16,2,1024]{2,1,0:T(2,128)(2,1)S(1)}, u32[]{:S(2)}, u32[]{:S(2)}) async-start(bf16[16,2,1024]{2,1,0:T(2,128)(2,1)} %get-tuple-element.6), calls=%async_computation.7 | async-start | bytes 131072 | tf_op jit(solution)/shard_map/all_to_all | solution.py:104
  198.1 60.5 %all-to-all-start.1 = ((bf16[16,2,256,256]{3,2,1,0:T(8,128)(2,1)}), bf16[16,2,256,256]{3,2,1,0:T(8,128)(2,1)}, u32[]{:S(2)}, u32[]{:S(2)}) async-start(bf16[16,2,256,256]{3,2,1,0:T(8,128)(2,1)} %broadcast_select_fusion), calls=%async_computation.1 | async-start | bytes 8388608 | tf_op jit(solution)/shard_map/all_to_all | solution.py:90
where the time goes:
time: 265 us; the launch traced here: 263 us
  waiting for transfers between devices  123 us (46%)
  local copies, waits for them, and re-layouts  50.7 us (19%)
  starting transfers between devices  34.7 us (13%)
  blocking collectives  24.4 us (9%)
  other arithmetic  16.4 us (6%)
  matrix products  13.6 us (5%)
    all_to_all x1, waiting for transfers between devices, move_results(): lax.all_to_all(jnp.take(spread[0], matching, axis=0), 'section', split_ax...  54.5 us
    all_to_all x1, waiting for transfers between devices, move_results(): lax.all_to_all(fold_rows(updated_cache, groups), 'section', split_axis=0,...  53.7 us
    all_to_all x1, blocking collectives, sum_at_owner(): lax.all_to_all(pieces, axis, split_axis=0, concat_axis=0, tiled=True)  24.4 us
    dot_general x1, local copies, waits for them, and re-layouts, decode_layer(): jnp.dot(attended, out_weight[0], preferred_element_type=jnp.float32)  22.4 us
    unnamed x17, local copies, waits for them, and re-layouts  13.1 us
    dot_general x1, matrix products, decode_layer(): jnp.dot(attended, out_weight[0], preferred_element_type=jnp.float32)  10.8 us
    select_n x2, other arithmetic, attend(): jnp.where(written[:, :, None], fresh_rows[:, None, :], cache_rows)  8.84 us
    all_to_all x1, starting transfers between devices, move_results(): lax.all_to_all(fold_rows(stream, groups), 'section', split_axis=0, concat...  7.78 us
  transfers between devices with their start and end apart: 7, of which 7 were waited for; matrix products, arithmetic and copies ran while one was open for 7% of the time, Pallas kernels for 0%

commit v1 on v0

v1 whole, which is shorter than its diff:
```python
import functools
import math

import jax
import jax.numpy as jnp
from jax import lax
from jax.experimental import pallas as pl
from jax.experimental.pallas import tpu as pltpu
from jax.sharding import PartitionSpec as P

MESH = pl.DeviceIdType.MESH
D = 8192
HEAD = 128
BATCH = 32
SLOTS = 256
GROUPS = 16
CHUNKS = 4
PER_CHUNK = SLOTS // CHUNKS
F32 = jnp.float32
BF16 = jnp.bfloat16

OFFSETS = []
for other_core in (0, 1):
    OFFSETS += [
        (1, 2, other_core), (0, 1, other_core), (1, 3, other_core), (0, 2, other_core),
        (1, 1, other_core), (0, 3, other_core), (1, 0, other_core),
    ]
OFFSETS += [(0, 0, 1)]
PARTNERS = len(OFFSETS)


def kernel(
    matching, lengths, queries, kv, fresh, residual, weight, gain,
    cache_out, stream_out, normed_out,
    cache, fresh32, attended, wide, partial, y_got, z_part, z_got, squares, sq_y, sq_z, sq_zs,
    mine, rows_got, rows_next, rows_last, got, nxt,
    load_sem, weight_sem, send1, recv1, send2, recv2, own_sem,
    y_send, y_recv, z_send, z_recv, sy_send, sy_recv, sz_send, sz_recv,
    rs1, rr1, rs2, rr2,
):
    me = lax.axis_index("section")
    zlo, x, core = me // 8, (me // 2) % 4, me % 2
    t = lax.axis_index("tensor")
    zhi, y = t // 4, t % 4
    partners = [
        ((zlo + dz) % 2) * 8 + ((x + dx) % 4) * 2 + (core + dc) % 2 for dz, dx, dc in OFFSETS
    ]
    y_partners = [zhi * 4 + (y + d) % 4 for d in (1, 2, 3)]
    z_partner = (1 - zhi) * 4 + y

    def to(src, dst, ss, rs, **where):
        return pltpu.make_async_remote_copy(
            src, dst, ss, rs, device_id=where, device_id_type=MESH
        )

    def load(q):
        rows = pl.ds(q * PER_CHUNK, PER_CHUNK)
        return pltpu.make_async_copy(kv.at[:, rows], cache.at[:, rows], load_sem.at[q])

    for q in range(CHUNKS):
        load(q).start()

    def block_of(n):
        return (n % 2) * 4 + (y + 1 + n // 2) % 4

    def load_weight(n):
        cols = pl.ds(pl.multiple_of(block_of(n) * 1024, 1024), 1024)
        return pltpu.make_async_copy(weight.at[:, cols], wide.at[n], weight_sem.at[n])

    for n in range(8):
        load_weight(n).start()

    barrier = pltpu.get_barrier_semaphore()
    for p in partners:
        pl.semaphore_signal(barrier, inc=1, device_id={"section": p}, device_id_type=MESH)
    for p in y_partners + [z_partner]:
        pl.semaphore_signal(barrier, inc=1, device_id={"tensor": p}, device_id_type=MESH)

    fresh32[...] = fresh[...].astype(F32)

    def spread(q, k):
        p = partners[k]
        return to(
            cache.at[pl.ds(2 * p, 2), pl.ds(q * PER_CHUNK, PER_CHUNK)], got[q].at[me],
            send1.at[q, k], recv1.at[q, k], section=p,
        )

    def keep(q):
        return pltpu.make_async_copy(
            cache.at[pl.ds(2 * me, 2), pl.ds(q * PER_CHUNK, PER_CHUNK)], got[q].at[me],
            own_sem.at[0, q],
        )

    for q in range(CHUNKS):
        load(q).wait()

        def write(b, _):
            rows = pl.ds(q * PER_CHUNK, PER_CHUNK)
            old = cache[b, rows, :].astype(F32)
            place = lax.broadcasted_iota(jnp.int32, (PER_CHUNK, 2 * HEAD), 0) + q * PER_CHUNK
            new = jnp.broadcast_to(fresh32[pl.ds(b, 1), :], old.shape)
            cache[b, rows, :] = jnp.where(place == lengths[b], new, old).astype(BF16)
            return 0

        lax.fori_loop(0, BATCH, write, 0)
        if q == 0:
            pl.semaphore_wait(barrier, PARTNERS + 4)
        for k in range(PARTNERS):
            spread(q, k).start()
        keep(q).start()

    def attend(b, _):
        keys, values = cache[b, :, :HEAD], cache[b, :, HEAD:]
        scores = lax.dot_general(
            queries[b], keys, (((1,), (1,)), ((), ())), preferred_element_type=F32
        ) * (1.0 / math.sqrt(HEAD))
        place = lax.broadcasted_iota(jnp.int32, scores.shape, 1)
        scores = jnp.where(place <= lengths[b], scores, -1e30)
        grown = jnp.exp(scores - jnp.max(scores, axis=1, keepdims=True))
        weights = (grown / jnp.sum(grown, axis=1, keepdims=True)).astype(BF16)
        result = jnp.dot(weights, values, preferred_element_type=F32)
        attended[pl.ds(pl.multiple_of(b * 8, 8), 8), :] = result.astype(BF16).astype(F32)
        return 0

    lax.fori_loop(0, BATCH, attend, 0)
    heads = jnp.concatenate(
        [attended[pl.ds(h, BATCH, stride=8), :].astype(BF16) for h in range(8)], axis=1
    )

    def y_part(i, z2):
        return to(
            partial.at[z2 * 4 + (y + 1 + i) % 4], y_got.at[i, z2],
            y_send.at[i, z2], y_recv.at[i, z2], tensor=y_partners[i],
        )

    for n in range(8):
        load_weight(n).wait()
        partial[block_of(n)] = jnp.dot(heads, wide[n], preferred_element_type=F32)
        if n < 6:
            y_part(n // 2, n % 2).start()

    def pass_on(q):
        return [
            to(
                nxt[q].at[partners[k]],
                cache_out.at[pl.ds(2 * me, 2), pl.ds(q * PER_CHUNK, PER_CHUNK)],
                send2.at[q, k], recv2.at[q, k], section=partners[k],
            )
            for k in range(PARTNERS)
        ]

    def leave(q):
        return pltpu.make_async_copy(
            nxt[q].at[me], cache_out.at[pl.ds(2 * me, 2), pl.ds(q * PER_CHUNK, PER_CHUNK)],
            own_sem.at[1, q],
        )

    def turn(q):
        keep(q).wait()
        for k in range(PARTNERS):
            spread(q, k).wait_recv()

        def pick(p, _):
            nxt[q][p] = got[q][matching[p]]
            return 0

        lax.fori_loop(0, GROUPS, pick, 0)
        for copy in pass_on(q):
            copy.start()
        leave(q).start()

    for i in range(3):
        for z2 in range(2):
            y_part(i, z2).wait_recv()
    z_part[...] = partial[(1 - zhi) * 4 + y] + (
        y_got[0, 1 - zhi] + y_got[1, 1 - zhi] + y_got[2, 1 - zhi]
    )
    z_copy = to(z_part, z_got, z_send, z_recv, tensor=z_partner)
    z_copy.start()
    stream = partial[zhi * 4 + y] + (y_got[0, zhi] + y_got[1, zhi] + y_got[2, zhi])
    z_copy.wait_recv()
    stream = stream + z_got[...] + residual[...].astype(F32)
    squares[...] = jnp.broadcast_to(
        jnp.sum(stream * stream, axis=1, keepdims=True), squares.shape
    )
    sq_copies = [
        to(squares, sq_y.at[i], sy_send.at[i], sy_recv.at[i], tensor=y_partners[i])
        for i in range(3)
    ]
    for copy in sq_copies:
        copy.start()
    for copy in sq_copies:
        copy.wait_recv()
    sq_zs[...] = squares[...] + (sq_y[0] + sq_y[1] + sq_y[2])
    sq_copy = to(sq_zs, sq_z, sz_send, sz_recv, tensor=z_partner)
    sq_copy.start()
    sq_copy.wait_recv()
    scale = lax.rsqrt((sq_zs[:, :1] + sq_z[:, :1]) / D + 1e-05)
    normed = (stream * scale * gain[...].astype(F32)).astype(BF16)
    stream = stream.astype(BF16)
    for j in range(GROUPS):
        r, c = (j // 8) * 16, (j % 8) * HEAD
        mine[j, 0] = stream[r : r + 16, c : c + HEAD]
        mine[j, 1] = normed[r : r + 16, c : c + HEAD]
    row_copies = [
        to(mine.at[p], rows_got.at[me], rs1.at[k], rr1.at[k], section=p)
        for k, p in enumerate(partners)
    ]
    for copy in row_copies:
        copy.start()
    rows_got[me] = mine[me]

    for q in range(CHUNKS - 1):
        turn(q)

    for copy in row_copies:
        copy.wait_recv()

    def pick_rows(p, _):
        rows_next[p] = rows_got[matching[p]]
        return 0

    lax.fori_loop(0, GROUPS, pick_rows, 0)
    row_copies2 = [
        to(rows_next.at[p], rows_last.at[me], rs2.at[k], rr2.at[k], section=p)
        for k, p in enumerate(partners)
    ]
    for copy in row_copies2:
        copy.start()
    rows_last[me] = rows_next[me]

    turn(CHUNKS - 1)

    for copy in row_copies2:
        copy.wait_recv()
    for j in range(GROUPS):
        r, c = (j // 8) * 16, (j % 8) * HEAD
        stream_out[r : r + 16, c : c + HEAD] = rows_last[j, 0]
        normed_out[r : r + 16, c : c + HEAD] = rows_last[j, 1]

    for i in range(3):
        for z2 in range(2):
            y_part(i, z2).wait_send()
    z_copy.wait_send()
    sq_copy.wait_send()
    for copy in sq_copies + row_copies + row_copies2:
        copy.wait_send()
    for q in range(CHUNKS):
        for k in range(PARTNERS):
            spread(q, k).wait_send()
    for q in range(CHUNKS):
        for copy in pass_on(q):
            copy.wait()
        leave(q).wait()


def on_device(
    matching, lengths, queries, kv_cache, incoming_key_value, residual, out_weight, norm_gain
):
    smem = pl.BlockSpec(memory_space=pltpu.SMEM)
    vmem = pl.BlockSpec(memory_space=pltpu.VMEM)
    anywhere = pl.BlockSpec(memory_space=pl.ANY)
    chunk = pltpu.VMEM((GROUPS, 2, PER_CHUNK, 2 * HEAD), BF16)
    rows = pltpu.VMEM((GROUPS, 2, 16, HEAD), BF16)
    dma = pltpu.SemaphoreType.DMA
    cache_out, stream_out, normed_out = pl.pallas_call(
        kernel,
        out_shape=(
            jax.ShapeDtypeStruct((BATCH, SLOTS, 2 * HEAD), BF16),
            jax.ShapeDtypeStruct((BATCH, 1024), BF16),
            jax.ShapeDtypeStruct((BATCH, 1024), BF16),
        ),
        in_specs=[smem, smem, vmem, anywhere, vmem, vmem, anywhere, vmem],
        out_specs=(anywhere, vmem, vmem),
        scratch_shapes=[
            pltpu.VMEM((BATCH, SLOTS, 2 * HEAD), BF16),
            pltpu.VMEM((BATCH, 2 * HEAD), F32),
            pltpu.VMEM((BATCH * 8, HEAD), F32),
            pltpu.VMEM((8, 1024, 1024), BF16),
            pltpu.VMEM((8, BATCH, 1024), F32),
            pltpu.VMEM((3, 2, BATCH, 1024), F32),
            pltpu.VMEM((BATCH, 1024), F32),
            pltpu.VMEM((BATCH, 1024), F32),
            pltpu.VMEM((BATCH, HEAD), F32),
            pltpu.VMEM((3, BATCH, HEAD), F32),
            pltpu.VMEM((BATCH, HEAD), F32),
            pltpu.VMEM((BATCH, HEAD), F32),
            rows, rows, rows, rows,
            [chunk] * CHUNKS,
            [chunk] * CHUNKS,
            dma((CHUNKS,)), dma((8,)),
            dma((CHUNKS, PARTNERS)), dma((CHUNKS, PARTNERS)),
            dma((CHUNKS, PARTNERS)), dma((CHUNKS, PARTNERS)),
            dma((2, CHUNKS)),
            dma((3, 2)), dma((3, 2)), dma, dma,
            dma((3,)), dma((3,)), dma, dma,
            dma((PARTNERS,)), dma((PARTNERS,)), dma((PARTNERS,)), dma((PARTNERS,)),
        ],
        compiler_params=pltpu.CompilerParams(
            collective_id=0, has_side_effects=True, vmem_limit_bytes=56 << 20
        ),
    )(
        matching, lengths, queries.reshape(BATCH, 8, HEAD), kv_cache[0], incoming_key_value[0],
        residual[0], out_weight[0], norm_gain,
    )
    return cache_out[None], stream_out[None], normed_out[None]


def solution(mesh):
    return jax.shard_map(
        on_device,
        mesh=mesh,
        in_specs=(
            P(),
            P(),
            P("section", None, "tensor"),
            P("section", None, None, "tensor"),
            P("section", None, "tensor"),
            P("section", None, "tensor"),
            P("section", "tensor", None),
            P("section", "tensor"),
        ),
        out_specs=(
            P("section", None, None, "tensor"),
            P("section", None, "tensor"),
            P("section", None, "tensor"),
        ),
        check_vma=False,
    )
```

time: 265 us -> 128 us (0.48)
  waiting for transfers between devices: 123 us -> 0 us
  Pallas kernels: 0 us -> 120 us
  local copies, waits for them, and re-layouts: 50.7 us -> 7.42 us
  starting transfers between devices: 34.7 us -> 0 us
  blocking collectives: 24.4 us -> 0 us
  other arithmetic: 16.4 us -> 0 us
  matrix products: 13.6 us -> 0 us
    all_to_all x7 -> x0, waiting for transfers between devices: 123 us -> none  [the longest x1 54.5 us: move_results(): lax.all_to_all(jnp.take(spread[0], matching, axis=0), 'section', split_ax...]
    pallas_call x0 -> x1, Pallas kernels: none -> 120 us  [on_device(): pl.pallas_call(kernel, out_shape=(jax.ShapeDtypeStruct((BATCH, SLOTS, 2 *...]
    all_to_all x7 -> x0, starting transfers between devices: 34.7 us -> none  [the longest x1 7.78 us: move_results(): lax.all_to_all(fold_rows(stream, groups), 'section', split_axis=0, concat...]
    all_to_all x1 -> x0, blocking collectives: 24.4 us -> none  [sum_at_owner(): lax.all_to_all(pieces, axis, split_axis=0, concat_axis=0, tiled=True)]
    dot_general x1 -> x0, local copies, waits for them, and re-layouts: 22.4 us -> none  [decode_layer(): jnp.dot(attended, out_weight[0], preferred_element_type=jnp.float32)]
    select_n x5 -> x0, other arithmetic: 14.3 us -> none  [the longest x2 8.84 us: attend(): jnp.where(written[:, :, None], fresh_rows[:, None, :], cache_rows)]
    dot_general x3 -> x0, matrix products: 13.6 us -> none  [the longest x1 10.8 us: decode_layer(): jnp.dot(attended, out_weight[0], preferred_element_type=jnp.float32)]
    squeeze x1 -> x0, local copies, waits for them, and re-layouts: 6.42 us -> none  [decode_layer(): kv_cache[0]]
  transfers between devices with their start and end apart: 7 -> 0, of which waited for: 7 -> 0; matrix products, arithmetic and copies ran while one was open for 7% -> 0% of each run, Pallas kernels for 0% -> 0%
where the time goes in v1:
time: 128 us
  Pallas kernels  120 us (94%)
  local copies, waits for them, and re-layouts  7.42 us (6%)
    pallas_call x1, Pallas kernels, on_device(): pl.pallas_call(kernel, out_shape=(jax.ShapeDtypeStruct((BATCH, SLOTS, 2 *...  120 us
    unnamed x8, local copies, waits for them, and re-layouts  7.42 us

profile of v1, /device:TPU:1, one launch (start us, length us, event | category | flops | bytes accessed | tf_op | source)
XLA Modules:
  0.0 127.6 jit_solution(10918219252765978007)
XLA Ops:
  0.6 1.5 %copy.11 = bf16[4,8,8,128]{3,2,1,0:T(8,128)(2,1)} copy(bf16[4,8,8,128]{3,1,2,0:T(8,128)(2,1)} %bitcast.15) | data formatting | bytes 131072
  2.1 119.5 %shard_map.103 = (bf16[32,256,256]{2,1,0:T(8,128)(2,1)}, bf16[32,1024]{1,0:T(8,128)(2,1)}, bf16[32,1024]{1,0:T(8,128)(2,1)}) custom-call(s32[16]{0:T(128)} %matching.1, s32[32]{0:T(128)} %lengths.1, bf16[32,8,128]{2,1,0:T(8,128)(2,1)} %bitcast.13, bf16[32,256,256]{2,1,0:T(8,128)(2,1)} %bitcast.11, bf16[32,256]{1,0:T(8,128)(2,1)} %bitcast.18, ...), custom_call_target="tpu_custom_call" | custom-call | tf_op jit(solution)/shard_map/pallas_call | solution.py:266
  121.6 0.0 copy-start.1
  121.6 0.0 copy-start
  121.6 4.7 %copy.15 = bf16[1,32,256,256]{3,2,1,0:T(8,128)(2,1)} copy(bf16[1,32,256,256]{3,2,1,0:T(8,128)(2,1)} %bitcast.12) | data formatting | bytes 8388608
  126.3 0.0 copy-done.1
  126.3 0.6 copy.16
  127.0 0.0 copy-done
  127.0 0.6 copy.17
Async XLA Ops:
  121.6 4.7 %copy-start.1 = (bf16[32,1024]{1,0:T(8,128)(2,1)S(1)}, bf16[32,1024]{1,0:T(8,128)(2,1)}, u32[]{:S(2)}) copy-start(bf16[32,1024]{1,0:T(8,128)(2,1)} %get-tuple-element.7) | copy-start | bytes 196612
  121.6 5.3 %copy-start = (bf16[32,1024]{1,0:T(8,128)(2,1)S(1)}, bf16[32,1024]{1,0:T(8,128)(2,1)}, u32[]{:S(2)}) copy-start(bf16[32,1024]{1,0:T(8,128)(2,1)} %get-tuple-element.8) | copy-start | bytes 196612

commit v2 on v1

--- a/solution.py
+++ b/solution.py
@@ -31,9 +31,9 @@
 
 def kernel(
     matching, lengths, queries, kv, fresh, residual, weight, gain,
-    cache_out, stream_out, normed_out,
-    cache, fresh32, attended, wide, partial, y_got, z_part, z_got, squares, sq_y, sq_z, sq_zs,
-    mine, rows_got, rows_next, rows_last, got, nxt,
+    cache_out, rows_out,
+    cache, fresh32, asked, attended, wide, partial, y_got, z_part, z_got, squares, sq_y, sq_z, sq_zs,
+    mine, rows_got, rows_next, got, nxt,
     load_sem, weight_sem, send1, recv1, send2, recv2, own_sem,
     y_send, y_recv, z_send, z_recv, sy_send, sy_recv, sz_send, sz_recv,
     rs1, rr1, rs2, rr2,
@@ -53,76 +53,77 @@
             src, dst, ss, rs, device_id=where, device_id_type=MESH
         )
 
-    def load(q):
-        rows = pl.ds(q * PER_CHUNK, PER_CHUNK)
-        return pltpu.make_async_copy(kv.at[:, rows], cache.at[:, rows], load_sem.at[q])
-
-    for q in range(CHUNKS):
-        load(q).start()
-
-    def block_of(n):
-        return (n % 2) * 4 + (y + 1 + n // 2) % 4
-
-    def load_weight(n):
-        cols = pl.ds(pl.multiple_of(block_of(n) * 1024, 1024), 1024)
-        return pltpu.make_async_copy(weight.at[:, cols], wide.at[n], weight_sem.at[n])
-
-    for n in range(8):
-        load_weight(n).start()
-
     barrier = pltpu.get_barrier_semaphore()
     for p in partners:
         pl.semaphore_signal(barrier, inc=1, device_id={"section": p}, device_id_type=MESH)
     for p in y_partners + [z_partner]:
         pl.semaphore_signal(barrier, inc=1, device_id={"tensor": p}, device_id_type=MESH)
 
-    fresh32[...] = fresh[...].astype(F32)
+    load = pltpu.make_async_copy(kv, cache, load_sem)
+    load.start()
+
+    def block_of(n):
+        return (n % 2) * 4 + (y + 1 + n // 2) % 4
+
+    def load_weight(n):
+        cols = pl.ds(pl.multiple_of(block_of(n) * 1024, 1024), 1024)
+        return pltpu.make_async_copy(weight.at[:, cols], wide.at[n], weight_sem.at[n])
 
     def spread(q, k):
         p = partners[k]
         return to(
-            cache.at[pl.ds(2 * p, 2), pl.ds(q * PER_CHUNK, PER_CHUNK)], got[q].at[me],
+            kv.at[pl.ds(2 * p, 2), pl.ds(q * PER_CHUNK, PER_CHUNK)], got[q].at[me],
             send1.at[q, k], recv1.at[q, k], section=p,
         )
 
     def keep(q):
         return pltpu.make_async_copy(
-            cache.at[pl.ds(2 * me, 2), pl.ds(q * PER_CHUNK, PER_CHUNK)], got[q].at[me],
+            kv.at[pl.ds(2 * me, 2), pl.ds(q * PER_CHUNK, PER_CHUNK)], got[q].at[me],
             own_sem.at[0, q],
         )
 
-    for q in range(CHUNKS):
-        load(q).wait()
-
-        def write(b, _):
-            rows = pl.ds(q * PER_CHUNK, PER_CHUNK)
-            old = cache[b, rows, :].astype(F32)
-            place = lax.broadcasted_iota(jnp.int32, (PER_CHUNK, 2 * HEAD), 0) + q * PER_CHUNK
-            new = jnp.broadcast_to(fresh32[pl.ds(b, 1), :], old.shape)
-            cache[b, rows, :] = jnp.where(place == lengths[b], new, old).astype(BF16)
-            return 0
-
-        lax.fori_loop(0, BATCH, write, 0)
-        if q == 0:
-            pl.semaphore_wait(barrier, PARTNERS + 4)
+    def spread_all(q):
         for k in range(PARTNERS):
             spread(q, k).start()
         keep(q).start()
 
-    def attend(b, _):
+    pl.semaphore_wait(barrier, PARTNERS + 4)
+    spread_all(0)
+    for n in range(8):
+        load_weight(n).start()
+    for q in range(1, CHUNKS):
+        spread_all(q)
+
+    fresh32[...] = fresh[...].astype(F32)
+    for h in range(8):
+        asked[pl.ds(h, BATCH, stride=8), :] = queries[:, h * HEAD : (h + 1) * HEAD].astype(F32)
+    load.wait()
+
+    def attend(b):
+        query = asked[pl.ds(pl.multiple_of(b * 8, 8), 8), :]
         keys, values = cache[b, :, :HEAD], cache[b, :, HEAD:]
+        newest = fresh32[pl.ds(b, 1), :]
+        new_key, new_value = newest[:, :HEAD], newest[:, HEAD:]
         scores = lax.dot_general(
-            queries[b], keys, (((1,), (1,)), ((), ())), preferred_element_type=F32
-        ) * (1.0 / math.sqrt(HEAD))
+            query.astype(BF16), keys, (((1,), (1,)), ((), ())), preferred_element_type=F32
+        )
         place = lax.broadcasted_iota(jnp.int32, scores.shape, 1)
+        own = jnp.sum(query * new_key, axis=1, keepdims=True)
+        scores = jnp.where(place == lengths[b], own, scores) * (1.0 / math.sqrt(HEAD))
         scores = jnp.where(place <= lengths[b], scores, -1e30)
         grown = jnp.exp(scores - jnp.max(scores, axis=1, keepdims=True))
-        weights = (grown / jnp.sum(grown, axis=1, keepdims=True)).astype(BF16)
-        result = jnp.dot(weights, values, preferred_element_type=F32)
+        weights = (grown / jnp.sum(grown, axis=1, keepdims=True)).astype(BF16).astype(F32)
+        old = jnp.where(place == lengths[b], 0.0, weights)
+        result = jnp.dot(old.astype(BF16), values, preferred_element_type=F32)
+        result = result + jnp.sum(weights - old, axis=1, keepdims=True) * new_value
         attended[pl.ds(pl.multiple_of(b * 8, 8), 8), :] = result.astype(BF16).astype(F32)
+
+    def attend_some(i, _):
+        for j in range(4):
+            attend(i * 4 + j)
         return 0
 
-    lax.fori_loop(0, BATCH, attend, 0)
+    lax.fori_loop(0, BATCH // 4, attend_some, 0)
     heads = jnp.concatenate(
         [attended[pl.ds(h, BATCH, stride=8), :].astype(BF16) for h in range(8)], axis=1
     )
@@ -169,6 +170,7 @@
             copy.start()
         leave(q).start()
 
+    turn(0)
     for i in range(3):
         for z2 in range(2):
             y_part(i, z2).wait_recv()
@@ -178,6 +180,7 @@
     z_copy = to(z_part, z_got, z_send, z_recv, tensor=z_partner)
     z_copy.start()
     stream = partial[zhi * 4 + y] + (y_got[0, zhi] + y_got[1, zhi] + y_got[2, zhi])
+    turn(1)
     z_copy.wait_recv()
     stream = stream + z_got[...] + residual[...].astype(F32)
     squares[...] = jnp.broadcast_to(
@@ -194,14 +197,18 @@
     sq_zs[...] = squares[...] + (sq_y[0] + sq_y[1] + sq_y[2])
     sq_copy = to(sq_zs, sq_z, sz_send, sz_recv, tensor=z_partner)
     sq_copy.start()
+    turn(2)
     sq_copy.wait_recv()
     scale = lax.rsqrt((sq_zs[:, :1] + sq_z[:, :1]) / D + 1e-05)
     normed = (stream * scale * gain[...].astype(F32)).astype(BF16)
     stream = stream.astype(BF16)
+    filler = jnp.zeros((12, HEAD), F32)
     for j in range(GROUPS):
         r, c = (j // 8) * 16, (j % 8) * HEAD
         mine[j, 0] = stream[r : r + 16, c : c + HEAD]
         mine[j, 1] = normed[r : r + 16, c : c + HEAD]
+        pair = fresh32[2 * j : 2 * j + 2, :]
+        mine[j, 2] = jnp.concatenate([pair[:, :HEAD], pair[:, HEAD:], filler], axis=0).astype(BF16)
     row_copies = [
         to(mine.at[p], rows_got.at[me], rs1.at[k], rr1.at[k], section=p)
         for k, p in enumerate(partners)
@@ -210,8 +217,7 @@
         copy.start()
     rows_got[me] = mine[me]
 
-    for q in range(CHUNKS - 1):
-        turn(q)
+    turn(CHUNKS - 1)
 
     for copy in row_copies:
         copy.wait_recv()
@@ -222,28 +228,19 @@
 
     lax.fori_loop(0, GROUPS, pick_rows, 0)
     row_copies2 = [
-        to(rows_next.at[p], rows_last.at[me], rs2.at[k], rr2.at[k], section=p)
+        to(rows_next.at[p], rows_out.at[me], rs2.at[k], rr2.at[k], section=p)
         for k, p in enumerate(partners)
     ]
     for copy in row_copies2:
         copy.start()
-    rows_last[me] = rows_next[me]
-
-    turn(CHUNKS - 1)
-
-    for copy in row_copies2:
-        copy.wait_recv()
-    for j in range(GROUPS):
-        r, c = (j // 8) * 16, (j % 8) * HEAD
-        stream_out[r : r + 16, c : c + HEAD] = rows_last[j, 0]
-        normed_out[r : r + 16, c : c + HEAD] = rows_last[j, 1]
+    rows_out[me] = rows_next[me]
 
     for i in range(3):
         for z2 in range(2):
             y_part(i, z2).wait_send()
     z_copy.wait_send()
     sq_copy.wait_send()
-    for copy in sq_copies + row_copies + row_copies2:
+    for copy in sq_copies + row_copies:
         copy.wait_send()
     for q in range(CHUNKS):
         for k in range(PARTNERS):
@@ -252,6 +249,32 @@
         for copy in pass_on(q):
             copy.wait()
         leave(q).wait()
+    for copy in row_copies2:
+        copy.wait()
+
+
+STEP = 4
+
+
+def finish(lengths, moved, rows, cache_out, stream_out, normed_out):
+    i = pl.program_id(0)
+
+    @pl.when(i == 0)
+    def _():
+        for j in range(GROUPS):
+            r, c = (j // 8) * 16, (j % 8) * HEAD
+            stream_out[r : r + 16, c : c + HEAD] = rows[j, 0]
+            normed_out[r : r + 16, c : c + HEAD] = rows[j, 1]
+
+    place = lax.broadcasted_iota(jnp.int32, (SLOTS, HEAD), 0).astype(F32).astype(BF16)
+    for b in range(STEP):
+        new = rows[i * (STEP // 2) + b // 2, 2].astype(F32)
+        here = place == lengths[i * STEP + b].astype(F32).astype(BF16)
+        for half in range(2):
+            row = 2 * half + b % 2
+            new_row = jnp.broadcast_to(new[row : row + 1, :].astype(BF16), (SLOTS, HEAD))
+            cols = slice(half * HEAD, (half + 1) * HEAD)
+            cache_out[b, :, cols] = jnp.where(here, new_row, moved[b, :, cols])
 
 
 def on_device(
@@ -261,20 +284,20 @@
     vmem = pl.BlockSpec(memory_space=pltpu.VMEM)
     anywhere = pl.BlockSpec(memory_space=pl.ANY)
     chunk = pltpu.VMEM((GROUPS, 2, PER_CHUNK, 2 * HEAD), BF16)
-    rows = pltpu.VMEM((GROUPS, 2, 16, HEAD), BF16)
+    rows = pltpu.VMEM((GROUPS, 3, 16, HEAD), BF16)
     dma = pltpu.SemaphoreType.DMA
-    cache_out, stream_out, normed_out = pl.pallas_call(
+    moved, rows_moved = pl.pallas_call(
         kernel,
         out_shape=(
             jax.ShapeDtypeStruct((BATCH, SLOTS, 2 * HEAD), BF16),
-            jax.ShapeDtypeStruct((BATCH, 1024), BF16),
-            jax.ShapeDtypeStruct((BATCH, 1024), BF16),
+            jax.ShapeDtypeStruct((GROUPS, 3, 16, HEAD), BF16),
         ),
         in_specs=[smem, smem, vmem, anywhere, vmem, vmem, anywhere, vmem],
-        out_specs=(anywhere, vmem, vmem),
+        out_specs=(anywhere, vmem),
         scratch_shapes=[
             pltpu.VMEM((BATCH, SLOTS, 2 * HEAD), BF16),
             pltpu.VMEM((BATCH, 2 * HEAD), F32),
+            pltpu.VMEM((BATCH * 8, HEAD), F32),
             pltpu.VMEM((BATCH * 8, HEAD), F32),
             pltpu.VMEM((8, 1024, 1024), BF16),
             pltpu.VMEM((8, BATCH, 1024), F32),
@@ -285,10 +308,10 @@
             pltpu.VMEM((3, BATCH, HEAD), F32),
             pltpu.VMEM((BATCH, HEAD), F32),
             pltpu.VMEM((BATCH, HEAD), F32),
-            rows, rows, rows, rows,
+            rows, rows, rows,
             [chunk] * CHUNKS,
             [chunk] * CHUNKS,
-            dma((CHUNKS,)), dma((8,)),
+            dma, dma((8,)),
             dma((CHUNKS, PARTNERS)), dma((CHUNKS, PARTNERS)),
             dma((CHUNKS, PARTNERS)), dma((CHUNKS, PARTNERS)),
             dma((2, CHUNKS)),
@@ -300,9 +323,22 @@
             collective_id=0, has_side_effects=True, vmem_limit_bytes=56 << 20
         ),
     )(
-        matching, lengths, queries.reshape(BATCH, 8, HEAD), kv_cache[0], incoming_key_value[0],
+        matching, lengths, queries[0], kv_cache[0], incoming_key_value[0],
         residual[0], out_weight[0], norm_gain,
     )
+    whole = pl.BlockSpec((BATCH, 1024), lambda i: (0, 0))
+    block = pl.BlockSpec((STEP, SLOTS, 2 * HEAD), lambda i: (i, 0, 0))
+    cache_out, stream_out, normed_out = pl.pallas_call(
+        finish,
+        out_shape=(
+            jax.ShapeDtypeStruct((BATCH, SLOTS, 2 * HEAD), BF16),
+            jax.ShapeDtypeStruct((BATCH, 1024), BF16),
+            jax.ShapeDtypeStruct((BATCH, 1024), BF16),
+        ),
+        grid=(BATCH // STEP,),
+        in_specs=[smem, block, pl.BlockSpec((GROUPS, 3, 16, HEAD), lambda i: (0, 0, 0, 0))],
+        out_specs=(block, whole, whole),
+    )(lengths, moved, rows_moved)
     return cache_out[None], stream_out[None], normed_out[None]
 
 

time: 128 us -> 121 us (0.945)
  local copies, waits for them, and re-layouts: 7.42 us -> 0 us
    unnamed x8 -> x0, local copies, waits for them, and re-layouts: 7.42 us -> none
    pallas_call x0 -> x1, Pallas kernels: none -> 6.95 us  [on_device(): pl.pallas_call(finish, out_shape=(jax.ShapeDtypeStruct((BATCH, SLOTS, 2 *...]
    pallas_call x1, Pallas kernels: 120 us -> 113 us  [on_device(): pl.pallas_call(kernel, out_shape=(jax.ShapeDtypeStruct((BATCH, SLOTS, 2 *...]
where the time goes in v2:
time: 121 us
  Pallas kernels  120 us (99%)
    pallas_call x1, Pallas kernels, on_device(): pl.pallas_call(kernel, out_shape=(jax.ShapeDtypeStruct((BATCH, SLOTS, 2 *...  113 us
    pallas_call x1, Pallas kernels, on_device(): pl.pallas_call(finish, out_shape=(jax.ShapeDtypeStruct((BATCH, SLOTS, 2 *...  6.95 us

profile of v2, /device:TPU:1, one launch (start us, length us, event | category | flops | bytes accessed | tf_op | source)
XLA Modules:
  0.0 121.0 jit_solution(12720224037029279137)
XLA Ops:
  0.6 113.4 %shard_map.103 = (bf16[32,256,256]{2,1,0:T(8,128)(2,1)}, bf16[16,3,16,128]{3,2,1,0:T(8,128)(2,1)}) custom-call(s32[16]{0:T(128)} %matching.1, s32[32]{0:T(128)} %lengths.3, bf16[32,1024]{1,0:T(8,128)(2,1)} %bitcast.10, bf16[32,256,256]{2,1,0:T(8,128)(2,1)} %bitcast.9, bf16[32,256]{1,0:T(8,128)(2,1)} %bitcast.12, bf16[32,1024]{1,0:T(8,128)(2,1)} %bitcast.11, ...), custom_call_target="tpu_custom_call" | custom-call | tf_op jit(solution)/shard_map/pallas_call | solution.py:289
  114.0 7.0 %shard_map.104 = (bf16[32,256,256]{2,1,0:T(8,128)(2,1)}, bf16[32,1024]{1,0:T(8,128)(2,1)}, bf16[32,1024]{1,0:T(8,128)(2,1)}) custom-call(s32[32]{0:T(128)} %lengths.3, bf16[32,256,256]{2,1,0:T(8,128)(2,1)} %get-tuple-element.8.moved, bf16[16,3,16,128]{3,2,1,0:T(8,128)(2,1)} %get-tuple-element.9.rows), custom_call_target="tpu_custom_call" | custom-call | tf_op jit(solution)/shard_map/pallas_call | solution.py:331

commit v3 on v2

--- a/solution.py
+++ b/solution.py
@@ -30,13 +30,14 @@
 
 
 def kernel(
-    matching, lengths, queries, kv, fresh, residual, weight, gain,
-    cache_out, rows_out,
-    cache, fresh32, asked, attended, wide, partial, y_got, z_part, z_got, squares, sq_y, sq_z, sq_zs,
-    mine, rows_got, rows_next, got, nxt,
-    load_sem, weight_sem, send1, recv1, send2, recv2, own_sem,
-    y_send, y_recv, z_send, z_recv, sy_send, sy_recv, sz_send, sz_recv,
-    rs1, rr1, rs2, rr2,
+    matching, lengths, queries_in, kv, fresh_in, residual_in, weight, gain_in,
+    cache_out, rows_out, new_out,
+    queries, fresh, residual, gain,
+    cache, fresh32, asked, attended, wide, partial, y_got, z_part, z_got, stream32, squares, sq_got,
+    mine, rows_got, rows_next, new_mine, new_got, new_next, got, nxt,
+    small_sem, load_sem, weight_sem, send1, recv1, send2, recv2, own_sem,
+    y_send, y_recv, z_send, z_recv, sq_send, sq_recv,
+    rs1, rr1, rs2, rr2, ns1, nr1, ns2, nr2,
 ):
     me = lax.axis_index("section")
     zlo, x, core = me // 8, (me // 2) % 4, me % 2
@@ -47,6 +48,7 @@
     ]
     y_partners = [zhi * 4 + (y + d) % 4 for d in (1, 2, 3)]
     z_partner = (1 - zhi) * 4 + y
+    t_partners = y_partners + [z_partner] + [(1 - zhi) * 4 + (y + d) % 4 for d in (1, 2, 3)]
 
     def to(src, dst, ss, rs, **where):
         return pltpu.make_async_remote_copy(
@@ -56,10 +58,18 @@
     barrier = pltpu.get_barrier_semaphore()
     for p in partners:
         pl.semaphore_signal(barrier, inc=1, device_id={"section": p}, device_id_type=MESH)
-    for p in y_partners + [z_partner]:
+    for p in t_partners:
         pl.semaphore_signal(barrier, inc=1, device_id={"tensor": p}, device_id_type=MESH)
 
     load = pltpu.make_async_copy(kv, cache, load_sem)
+    small = [
+        pltpu.make_async_copy(src, dst, small_sem.at[i])
+        for i, (src, dst) in enumerate(
+            [(queries_in, queries), (fresh_in, fresh), (residual_in, residual), (gain_in, gain)]
+        )
+    ]
+    for copy in small:
+        copy.start()
     load.start()
 
     def block_of(n):
@@ -87,14 +97,26 @@
             spread(q, k).start()
         keep(q).start()
 
-    pl.semaphore_wait(barrier, PARTNERS + 4)
+    pl.semaphore_wait(barrier, PARTNERS + 7)
     spread_all(0)
+    for copy in small:
+        copy.wait()
+    fresh32[...] = fresh[...].astype(F32)
+    for j in range(GROUPS):
+        pair = fresh32[2 * j : 2 * j + 2, :]
+        new_mine[j] = jnp.concatenate([pair[:, :HEAD], pair[:, HEAD:]], axis=0).astype(BF16)
+    new_copies = [
+        to(new_mine.at[p], new_got.at[me], ns1.at[k], nr1.at[k], section=p)
+        for k, p in enumerate(partners)
+    ]
+    for copy in new_copies:
+        copy.start()
+    new_got[me] = new_mine[me]
     for n in range(8):
         load_weight(n).start()
-    for q in range(1, CHUNKS):
+    for q in range(1, 3):
         spread_all(q)
 
-    fresh32[...] = fresh[...].astype(F32)
     for h in range(8):
         asked[pl.ds(h, BATCH, stride=8), :] = queries[:, h * HEAD : (h + 1) * HEAD].astype(F32)
     load.wait()
@@ -170,77 +192,109 @@
             copy.start()
         leave(q).start()
 
-    turn(0)
-    for i in range(3):
-        for z2 in range(2):
-            y_part(i, z2).wait_recv()
-    z_part[...] = partial[(1 - zhi) * 4 + y] + (
-        y_got[0, 1 - zhi] + y_got[1, 1 - zhi] + y_got[2, 1 - zhi]
-    )
     z_copy = to(z_part, z_got, z_send, z_recv, tensor=z_partner)
-    z_copy.start()
-    stream = partial[zhi * 4 + y] + (y_got[0, zhi] + y_got[1, zhi] + y_got[2, zhi])
-    turn(1)
-    z_copy.wait_recv()
-    stream = stream + z_got[...] + residual[...].astype(F32)
-    squares[...] = jnp.broadcast_to(
-        jnp.sum(stream * stream, axis=1, keepdims=True), squares.shape
-    )
     sq_copies = [
-        to(squares, sq_y.at[i], sy_send.at[i], sy_recv.at[i], tensor=y_partners[i])
-        for i in range(3)
-    ]
-    for copy in sq_copies:
-        copy.start()
-    for copy in sq_copies:
-        copy.wait_recv()
-    sq_zs[...] = squares[...] + (sq_y[0] + sq_y[1] + sq_y[2])
-    sq_copy = to(sq_zs, sq_z, sz_send, sz_recv, tensor=z_partner)
-    sq_copy.start()
-    turn(2)
-    sq_copy.wait_recv()
-    scale = lax.rsqrt((sq_zs[:, :1] + sq_z[:, :1]) / D + 1e-05)
-    normed = (stream * scale * gain[...].astype(F32)).astype(BF16)
-    stream = stream.astype(BF16)
-    filler = jnp.zeros((12, HEAD), F32)
-    for j in range(GROUPS):
-        r, c = (j // 8) * 16, (j % 8) * HEAD
-        mine[j, 0] = stream[r : r + 16, c : c + HEAD]
-        mine[j, 1] = normed[r : r + 16, c : c + HEAD]
-        pair = fresh32[2 * j : 2 * j + 2, :]
-        mine[j, 2] = jnp.concatenate([pair[:, :HEAD], pair[:, HEAD:], filler], axis=0).astype(BF16)
+        to(squares, sq_got.at[i], sq_send.at[i], sq_recv.at[i], tensor=p)
+        for i, p in enumerate(t_partners)
+    ]
     row_copies = [
         to(mine.at[p], rows_got.at[me], rs1.at[k], rr1.at[k], section=p)
         for k, p in enumerate(partners)
     ]
-    for copy in row_copies:
-        copy.start()
-    rows_got[me] = mine[me]
-
-    turn(CHUNKS - 1)
-
-    for copy in row_copies:
-        copy.wait_recv()
-
-    def pick_rows(p, _):
-        rows_next[p] = rows_got[matching[p]]
-        return 0
-
-    lax.fori_loop(0, GROUPS, pick_rows, 0)
     row_copies2 = [
         to(rows_next.at[p], rows_out.at[me], rs2.at[k], rr2.at[k], section=p)
         for k, p in enumerate(partners)
     ]
-    for copy in row_copies2:
-        copy.start()
-    rows_out[me] = rows_next[me]
+
+    def sum_y():
+        for i in range(3):
+            for z2 in range(2):
+                y_part(i, z2).wait_recv()
+        other, own = 1 - zhi, zhi
+        z_part[...] = partial[other * 4 + y] + (y_got[0, other] + y_got[1, other] + y_got[2, other])
+        z_copy.start()
+        stream32[...] = partial[own * 4 + y] + (y_got[0, own] + y_got[1, own] + y_got[2, own])
+
+    def diagonal():
+        shape = (BATCH, HEAD)
+        return lax.broadcasted_iota(jnp.int32, shape, 0) == lax.broadcasted_iota(jnp.int32, shape, 1)
+
+    def sum_z():
+        z_copy.wait_recv()
+        stream = stream32[...] + z_got[...] + residual[...].astype(F32)
+        stream32[...] = stream
+        sums = jnp.broadcast_to(jnp.sum(stream * stream, axis=1, keepdims=True), (BATCH, HEAD))
+        line = jnp.sum(jnp.where(diagonal(), sums, 0.0), axis=0, keepdims=True)
+        squares[...] = jnp.broadcast_to(line, squares.shape)
+        for copy in sq_copies:
+            copy.start()
+
+    def norm():
+        for copy in sq_copies:
+            copy.wait_recv()
+        line = squares[...]
+        for i in range(7):
+            line = line + sq_got[i]
+        line = jnp.broadcast_to(line[:1], (BATCH, HEAD))
+        total = jnp.sum(jnp.where(diagonal(), line, 0.0), axis=1, keepdims=True)
+        scale = lax.rsqrt(total / D + 1e-05)
+        normed = (stream32[...] * scale * gain[...].astype(F32)).astype(BF16)
+        stream = stream32[...].astype(BF16)
+        for j in range(GROUPS):
+            r, c = (j // 8) * 16, (j % 8) * HEAD
+            mine[j, 0] = stream[r : r + 16, c : c + HEAD]
+            mine[j, 1] = normed[r : r + 16, c : c + HEAD]
+        for copy in row_copies:
+            copy.start()
+        rows_got[me] = mine[me]
+
+    new_copies2 = [
+        to(new_next.at[p], new_out.at[me], ns2.at[k], nr2.at[k], section=p)
+        for k, p in enumerate(partners)
+    ]
+
+    def turn_new():
+        for copy in new_copies:
+            copy.wait_recv()
+
+        def pick_new(p, _):
+            new_next[p] = new_got[matching[p]]
+            return 0
+
+        lax.fori_loop(0, GROUPS, pick_new, 0)
+        for copy in new_copies2:
+            copy.start()
+        new_out[me] = new_next[me]
+
+    def turn_rows():
+        for copy in row_copies:
+            copy.wait_recv()
+
+        def pick_rows(p, _):
+            rows_next[p] = rows_got[matching[p]]
+            return 0
+
+        lax.fori_loop(0, GROUPS, pick_rows, 0)
+        for copy in row_copies2:
+            copy.start()
+        rows_out[me] = rows_next[me]
+
+    sum_y()
+    spread_all(3)
+    turn(0)
+    turn_new()
+    sum_z()
+    turn(1)
+    norm()
+    turn(2)
+    turn_rows()
+    turn(3)
 
     for i in range(3):
         for z2 in range(2):
             y_part(i, z2).wait_send()
     z_copy.wait_send()
-    sq_copy.wait_send()
-    for copy in sq_copies + row_copies:
+    for copy in sq_copies + row_copies + new_copies:
         copy.wait_send()
     for q in range(CHUNKS):
         for k in range(PARTNERS):
@@ -249,14 +303,14 @@
         for copy in pass_on(q):
             copy.wait()
         leave(q).wait()
-    for copy in row_copies2:
+    for copy in row_copies2 + new_copies2:
         copy.wait()
 
 
-STEP = 4
-
-
-def finish(lengths, moved, rows, cache_out, stream_out, normed_out):
+STEP = 8
+
+
+def finish(lengths, moved, rows, newest, cache_out, stream_out, normed_out):
     i = pl.program_id(0)
 
     @pl.when(i == 0)
@@ -268,33 +322,41 @@
 
     place = lax.broadcasted_iota(jnp.int32, (SLOTS, HEAD), 0).astype(F32).astype(BF16)
     for b in range(STEP):
-        new = rows[i * (STEP // 2) + b // 2, 2].astype(F32)
+        new = newest[i * (STEP // 2) + b // 2].astype(F32)
         here = place == lengths[i * STEP + b].astype(F32).astype(BF16)
         for half in range(2):
             row = 2 * half + b % 2
             new_row = jnp.broadcast_to(new[row : row + 1, :].astype(BF16), (SLOTS, HEAD))
             cols = slice(half * HEAD, (half + 1) * HEAD)
-            cache_out[b, :, cols] = jnp.where(here, new_row, moved[b, :, cols])
+            cache_out[b, :, cols] = jnp.where(here, new_row, moved[i * STEP + b, :, cols])
 
 
 def on_device(
     matching, lengths, queries, kv_cache, incoming_key_value, residual, out_weight, norm_gain
 ):
     smem = pl.BlockSpec(memory_space=pltpu.SMEM)
+    stay = lambda array: pltpu.with_memory_space_constraint(array, pltpu.HBM)
     vmem = pl.BlockSpec(memory_space=pltpu.VMEM)
     anywhere = pl.BlockSpec(memory_space=pl.ANY)
+    hbm = pl.BlockSpec(memory_space=pltpu.HBM)
     chunk = pltpu.VMEM((GROUPS, 2, PER_CHUNK, 2 * HEAD), BF16)
-    rows = pltpu.VMEM((GROUPS, 3, 16, HEAD), BF16)
+    rows = pltpu.VMEM((GROUPS, 2, 16, HEAD), BF16)
+    new = pltpu.VMEM((GROUPS, 4, HEAD), BF16)
     dma = pltpu.SemaphoreType.DMA
-    moved, rows_moved = pl.pallas_call(
+    moved, rows_moved, new_moved = pl.pallas_call(
         kernel,
         out_shape=(
             jax.ShapeDtypeStruct((BATCH, SLOTS, 2 * HEAD), BF16),
-            jax.ShapeDtypeStruct((GROUPS, 3, 16, HEAD), BF16),
+            jax.ShapeDtypeStruct((GROUPS, 2, 16, HEAD), BF16),
+            jax.ShapeDtypeStruct((GROUPS, 4, HEAD), BF16),
         ),
-        in_specs=[smem, smem, vmem, anywhere, vmem, vmem, anywhere, vmem],
-        out_specs=(anywhere, vmem),
+        in_specs=[smem, smem] + [hbm] * 6,
+        out_specs=(anywhere, vmem, vmem),
         scratch_shapes=[
+            pltpu.VMEM((BATCH, 1024), BF16),
+            pltpu.VMEM((BATCH, 2 * HEAD), BF16),
+            pltpu.VMEM((BATCH, 1024), BF16),
+            pltpu.VMEM((1, 1024), BF16),
             pltpu.VMEM((BATCH, SLOTS, 2 * HEAD), BF16),
             pltpu.VMEM((BATCH, 2 * HEAD), F32),
             pltpu.VMEM((BATCH * 8, HEAD), F32),
@@ -304,27 +366,25 @@
             pltpu.VMEM((3, 2, BATCH, 1024), F32),
             pltpu.VMEM((BATCH, 1024), F32),
             pltpu.VMEM((BATCH, 1024), F32),
-            pltpu.VMEM((BATCH, HEAD), F32),
-            pltpu.VMEM((3, BATCH, HEAD), F32),
-            pltpu.VMEM((BATCH, HEAD), F32),
-            pltpu.VMEM((BATCH, HEAD), F32),
-            rows, rows, rows,
+            pltpu.VMEM((BATCH, 1024), F32),
+            pltpu.VMEM((8, HEAD), F32),
+            pltpu.VMEM((7, 8, HEAD), F32),
+            rows, rows, rows, new, new, new,
             [chunk] * CHUNKS,
             [chunk] * CHUNKS,
-            dma, dma((8,)),
+            dma((4,)), dma, dma((8,)),
             dma((CHUNKS, PARTNERS)), dma((CHUNKS, PARTNERS)),
             dma((CHUNKS, PARTNERS)), dma((CHUNKS, PARTNERS)),
             dma((2, CHUNKS)),
-            dma((3, 2)), dma((3, 2)), dma, dma,
-            dma((3,)), dma((3,)), dma, dma,
-            dma((PARTNERS,)), dma((PARTNERS,)), dma((PARTNERS,)), dma((PARTNERS,)),
+            dma((3, 2)), dma((3, 2)), dma, dma, dma((7,)), dma((7,)),
+            *([dma((PARTNERS,))] * 8),
         ],
         compiler_params=pltpu.CompilerParams(
-            collective_id=0, has_side_effects=True, vmem_limit_bytes=56 << 20
+            collective_id=0, has_side_effects=True, vmem_limit_bytes=34 << 20
         ),
     )(
-        matching, lengths, queries[0], kv_cache[0], incoming_key_value[0],
-        residual[0], out_weight[0], norm_gain,
+        stay(matching), stay(lengths), stay(queries[0]), stay(kv_cache[0]),
+        stay(incoming_key_value[0]), stay(residual[0]), stay(out_weight[0]), stay(norm_gain),
     )
     whole = pl.BlockSpec((BATCH, 1024), lambda i: (0, 0))
     block = pl.BlockSpec((STEP, SLOTS, 2 * HEAD), lambda i: (i, 0, 0))
@@ -336,9 +396,10 @@
             jax.ShapeDtypeStruct((BATCH, 1024), BF16),
         ),
         grid=(BATCH // STEP,),
-        in_specs=[smem, block, pl.BlockSpec((GROUPS, 3, 16, HEAD), lambda i: (0, 0, 0, 0))],
+        in_specs=[smem, vmem, vmem, vmem],
         out_specs=(block, whole, whole),
-    )(lengths, moved, rows_moved)
+        compiler_params=pltpu.CompilerParams(vmem_limit_bytes=12 << 20),
+    )(stay(lengths), moved, rows_moved, new_moved)
     return cache_out[None], stream_out[None], normed_out[None]
 
 

time: 121 us -> 114 us (0.942)
  Pallas kernels: 120 us -> 113 us
    pallas_call x1, Pallas kernels: 113 us -> 109 us  [on_device(): pl.pallas_call(kernel, out_shape=(jax.ShapeDtypeStruct((BATCH, SLOTS, 2 *...]
    pallas_call x1, Pallas kernels: 6.95 us -> 3.38 us  [on_device(): pl.pallas_call(finish, out_shape=(jax.ShapeDtypeStruct((BATCH, SLOTS, 2 *...]
where the time goes in v3:
time: 114 us; the launch traced here: 113 us
  Pallas kernels  113 us (99%)
    pallas_call x1, Pallas kernels, on_device(): pl.pallas_call(kernel, out_shape=(jax.ShapeDtypeStruct((BATCH, SLOTS, 2 *...  109 us
    pallas_call x1, Pallas kernels, on_device(): pl.pallas_call(finish, out_shape=(jax.ShapeDtypeStruct((BATCH, SLOTS, 2 *...  3.38 us

profile of v3, /device:TPU:1, one launch (start us, length us, event | category | flops | bytes accessed | tf_op | source)
XLA Modules:
  0.0 113.5 jit_solution(13167594894928402940)
XLA Ops:
  0.6 109.5 %shard_map.103 = (bf16[32,256,256]{2,1,0:T(8,128)(2,1)S(1)}, bf16[16,2,16,128]{3,2,1,0:T(8,128)(2,1)S(1)}, bf16[16,4,128]{2,1,0:T(4,128)(2,1)S(1)}) custom-call(s32[16]{0:T(128)} %matching.1, s32[32]{0:T(128)} %lengths.3, bf16[32,1024]{1,0:T(8,128)(2,1)} %bitcast.10, bf16[32,256,256]{2,1,0:T(8,128)(2,1)} %bitcast.9, bf16[32,256]{1,0:T(8,128)(2,1)} %bitcast.12, ...), custom_call_target="tpu_custom_call" | custom-call | tf_op jit(solution)/shard_map/pallas_call | solution.py:346
  110.1 3.4 %shard_map.104 = (bf16[32,256,256]{2,1,0:T(8,128)(2,1)}, bf16[32,1024]{1,0:T(8,128)(2,1)}, bf16[32,1024]{1,0:T(8,128)(2,1)}) custom-call(s32[32]{0:T(128)} %lengths.3, bf16[32,256,256]{2,1,0:T(8,128)(2,1)S(1)} %get-tuple-element.9.moved, bf16[16,2,16,128]{3,2,1,0:T(8,128)(2,1)S(1)} %get-tuple-element.10.rows, bf16[16,4,128]{2,1,0:T(4,128)(2,1)S(1)} %get-tuple-element.11.newest), custom_call_target="tpu_custom_call" | custom-call | tf_op jit(solution)/shard_map/pallas_call | solution.py:391

commit v4 on v3

--- a/solution.py
+++ b/solution.py
@@ -14,8 +14,8 @@
 BATCH = 32
 SLOTS = 256
 GROUPS = 16
-CHUNKS = 4
-PER_CHUNK = SLOTS // CHUNKS
+CUTS = (96, 96, 64)
+CHUNKS = len(CUTS)
 F32 = jnp.float32
 BF16 = jnp.bfloat16
 
@@ -27,6 +27,10 @@
     ]
 OFFSETS += [(0, 0, 1)]
 PARTNERS = len(OFFSETS)
+
+
+def slots(q):
+    return slice(sum(CUTS[:q]), sum(CUTS[: q + 1]))
 
 
 def kernel(
@@ -82,13 +86,13 @@
     def spread(q, k):
         p = partners[k]
         return to(
-            kv.at[pl.ds(2 * p, 2), pl.ds(q * PER_CHUNK, PER_CHUNK)], got[q].at[me],
+            kv.at[pl.ds(2 * p, 2), slots(q)], got[q].at[me],
             send1.at[q, k], recv1.at[q, k], section=p,
         )
 
     def keep(q):
         return pltpu.make_async_copy(
-            kv.at[pl.ds(2 * me, 2), pl.ds(q * PER_CHUNK, PER_CHUNK)], got[q].at[me],
+            kv.at[pl.ds(2 * me, 2), slots(q)], got[q].at[me],
             own_sem.at[0, q],
         )
 
@@ -114,7 +118,7 @@
     new_got[me] = new_mine[me]
     for n in range(8):
         load_weight(n).start()
-    for q in range(1, 3):
+    for q in range(1, 2):
         spread_all(q)
 
     for h in range(8):
@@ -166,7 +170,7 @@
         return [
             to(
                 nxt[q].at[partners[k]],
-                cache_out.at[pl.ds(2 * me, 2), pl.ds(q * PER_CHUNK, PER_CHUNK)],
+                cache_out.at[pl.ds(2 * me, 2), slots(q)],
                 send2.at[q, k], recv2.at[q, k], section=partners[k],
             )
             for k in range(PARTNERS)
@@ -174,7 +178,7 @@
 
     def leave(q):
         return pltpu.make_async_copy(
-            nxt[q].at[me], cache_out.at[pl.ds(2 * me, 2), pl.ds(q * PER_CHUNK, PER_CHUNK)],
+            nxt[q].at[me], cache_out.at[pl.ds(2 * me, 2), slots(q)],
             own_sem.at[1, q],
         )
 
@@ -211,7 +215,8 @@
             for z2 in range(2):
                 y_part(i, z2).wait_recv()
         other, own = 1 - zhi, zhi
-        z_part[...] = partial[other * 4 + y] + (y_got[0, other] + y_got[1, other] + y_got[2, other])
+        half = partial[other * 4 + y] + (y_got[0, other] + y_got[1, other] + y_got[2, other])
+        z_part[...] = half.astype(BF16)
         z_copy.start()
         stream32[...] = partial[own * 4 + y] + (y_got[0, own] + y_got[1, own] + y_got[2, own])
 
@@ -221,7 +226,7 @@
 
     def sum_z():
         z_copy.wait_recv()
-        stream = stream32[...] + z_got[...] + residual[...].astype(F32)
+        stream = stream32[...] + z_got[...].astype(F32) + residual[...].astype(F32)
         stream32[...] = stream
         sums = jnp.broadcast_to(jnp.sum(stream * stream, axis=1, keepdims=True), (BATCH, HEAD))
         line = jnp.sum(jnp.where(diagonal(), sums, 0.0), axis=0, keepdims=True)
@@ -280,15 +285,14 @@
         rows_out[me] = rows_next[me]
 
     sum_y()
-    spread_all(3)
-    turn(0)
+    spread_all(2)
     turn_new()
     sum_z()
+    turn(0)
+    norm()
     turn(1)
-    norm()
+    turn_rows()
     turn(2)
-    turn_rows()
-    turn(3)
 
     for i in range(3):
         for z2 in range(2):
@@ -307,28 +311,47 @@
         copy.wait()
 
 
-STEP = 8
-
-
-def finish(lengths, moved, rows, newest, cache_out, stream_out, normed_out):
-    i = pl.program_id(0)
-
-    @pl.when(i == 0)
-    def _():
-        for j in range(GROUPS):
-            r, c = (j // 8) * 16, (j % 8) * HEAD
-            stream_out[r : r + 16, c : c + HEAD] = rows[j, 0]
-            normed_out[r : r + 16, c : c + HEAD] = rows[j, 1]
+STEP = 2
+
+
+def finish(
+    lengths, moved, rows, newest, cache_out, stream_out, normed_out,
+    cache, stream, normed, sems, row_sems,
+):
+    for j in range(GROUPS):
+        r, c = (j // 8) * 16, (j % 8) * HEAD
+        stream[r : r + 16, c : c + HEAD] = rows[j, 0]
+        normed[r : r + 16, c : c + HEAD] = rows[j, 1]
+    row_copies = [
+        pltpu.make_async_copy(stream, stream_out, row_sems.at[0]),
+        pltpu.make_async_copy(normed, normed_out, row_sems.at[1]),
+    ]
+    for copy in row_copies:
+        copy.start()
+
+    def store(i):
+        part = pl.ds(i * STEP, STEP)
+        return pltpu.make_async_copy(cache.at[part], cache_out.at[part], sems.at[i])
 
     place = lax.broadcasted_iota(jnp.int32, (SLOTS, HEAD), 0).astype(F32).astype(BF16)
-    for b in range(STEP):
-        new = newest[i * (STEP // 2) + b // 2].astype(F32)
-        here = place == lengths[i * STEP + b].astype(F32).astype(BF16)
-        for half in range(2):
-            row = 2 * half + b % 2
-            new_row = jnp.broadcast_to(new[row : row + 1, :].astype(BF16), (SLOTS, HEAD))
-            cols = slice(half * HEAD, (half + 1) * HEAD)
-            cache_out[b, :, cols] = jnp.where(here, new_row, moved[i * STEP + b, :, cols])
+
+    def write(i, _):
+        for b in range(STEP):
+            new = newest[i * (STEP // 2) + b // 2].astype(F32)
+            here = place == lengths[i * STEP + b].astype(F32).astype(BF16)
+            for half in range(2):
+                row = 2 * half + b % 2
+                new_row = jnp.broadcast_to(new[row : row + 1, :].astype(BF16), (SLOTS, HEAD))
+                cols = slice(half * HEAD, (half + 1) * HEAD)
+                cache[i * STEP + b, :, cols] = jnp.where(here, new_row, moved[i * STEP + b, :, cols])
+        store(i).start()
+        return 0
+
+    lax.fori_loop(0, BATCH // STEP, write, 0)
+    for i in range(BATCH // STEP):
+        store(i).wait()
+    for copy in row_copies:
+        copy.wait()
 
 
 def on_device(
@@ -339,7 +362,7 @@
     vmem = pl.BlockSpec(memory_space=pltpu.VMEM)
     anywhere = pl.BlockSpec(memory_space=pl.ANY)
     hbm = pl.BlockSpec(memory_space=pltpu.HBM)
-    chunk = pltpu.VMEM((GROUPS, 2, PER_CHUNK, 2 * HEAD), BF16)
+    chunks = [pltpu.VMEM((GROUPS, 2, cut, 2 * HEAD), BF16) for cut in CUTS]
     rows = pltpu.VMEM((GROUPS, 2, 16, HEAD), BF16)
     new = pltpu.VMEM((GROUPS, 4, HEAD), BF16)
     dma = pltpu.SemaphoreType.DMA
@@ -364,14 +387,13 @@
             pltpu.VMEM((8, 1024, 1024), BF16),
             pltpu.VMEM((8, BATCH, 1024), F32),
             pltpu.VMEM((3, 2, BATCH, 1024), F32),
-            pltpu.VMEM((BATCH, 1024), F32),
-            pltpu.VMEM((BATCH, 1024), F32),
+            pltpu.VMEM((BATCH, 1024), BF16),
+            pltpu.VMEM((BATCH, 1024), BF16),
             pltpu.VMEM((BATCH, 1024), F32),
             pltpu.VMEM((8, HEAD), F32),
             pltpu.VMEM((7, 8, HEAD), F32),
             rows, rows, rows, new, new, new,
-            [chunk] * CHUNKS,
-            [chunk] * CHUNKS,
+            chunks, chunks,
             dma((4,)), dma, dma((8,)),
             dma((CHUNKS, PARTNERS)), dma((CHUNKS, PARTNERS)),
             dma((CHUNKS, PARTNERS)), dma((CHUNKS, PARTNERS)),
@@ -386,8 +408,6 @@
         stay(matching), stay(lengths), stay(queries[0]), stay(kv_cache[0]),
         stay(incoming_key_value[0]), stay(residual[0]), stay(out_weight[0]), stay(norm_gain),
     )
-    whole = pl.BlockSpec((BATCH, 1024), lambda i: (0, 0))
-    block = pl.BlockSpec((STEP, SLOTS, 2 * HEAD), lambda i: (i, 0, 0))
     cache_out, stream_out, normed_out = pl.pallas_call(
         finish,
         out_shape=(
@@ -395,9 +415,15 @@
             jax.ShapeDtypeStruct((BATCH, 1024), BF16),
             jax.ShapeDtypeStruct((BATCH, 1024), BF16),
         ),
-        grid=(BATCH // STEP,),
         in_specs=[smem, vmem, vmem, vmem],
-        out_specs=(block, whole, whole),
+        out_specs=(hbm, hbm, hbm),
+        scratch_shapes=[
+            pltpu.VMEM((BATCH, SLOTS, 2 * HEAD), BF16),
+            pltpu.VMEM((BATCH, 1024), BF16),
+            pltpu.VMEM((BATCH, 1024), BF16),
+            dma((BATCH // STEP,)),
+            dma((2,)),
+        ],
         compiler_params=pltpu.CompilerParams(vmem_limit_bytes=12 << 20),
     )(stay(lengths), moved, rows_moved, new_moved)
     return cache_out[None], stream_out[None], normed_out[None]

time: 114 us -> 112 us (0.982)
  Pallas kernels: 113 us -> 111 us
where the time goes in v4:
time: 112 us
  Pallas kernels  111 us (99%)
    pallas_call x1, Pallas kernels, on_device(): pl.pallas_call(kernel, out_shape=(jax.ShapeDtypeStruct((BATCH, SLOTS, 2 *...  108 us
    pallas_call x1, Pallas kernels, on_device(): pl.pallas_call(finish, out_shape=(jax.ShapeDtypeStruct((BATCH, SLOTS, 2 *...  2.9 us

profile of v4, /device:TPU:1, one launch (start us, length us, event | category | flops | bytes accessed | tf_op | source)
XLA Modules:
  0.0 111.9 jit_solution(1175656838070182194)
XLA Ops:
  0.6 108.4 %shard_map.103 = (bf16[32,256,256]{2,1,0:T(8,128)(2,1)S(1)}, bf16[16,2,16,128]{3,2,1,0:T(8,128)(2,1)S(1)}, bf16[16,4,128]{2,1,0:T(4,128)(2,1)S(1)}) custom-call(s32[16]{0:T(128)} %matching.1, s32[32]{0:T(128)} %lengths.3, bf16[32,1024]{1,0:T(8,128)(2,1)} %bitcast.10, bf16[32,256,256]{2,1,0:T(8,128)(2,1)} %bitcast.9, bf16[32,256]{1,0:T(8,128)(2,1)} %bitcast.12, ...), custom_call_target="tpu_custom_call" | custom-call | tf_op jit(solution)/shard_map/pallas_call | solution.py:369
  109.0 2.9 %shard_map.104 = (bf16[32,256,256]{2,1,0:T(8,128)(2,1)}, bf16[32,1024]{1,0:T(8,128)(2,1)}, bf16[32,1024]{1,0:T(8,128)(2,1)}) custom-call(s32[32]{0:T(128)} %lengths.3, bf16[32,256,256]{2,1,0:T(8,128)(2,1)S(1)} %get-tuple-element.9.moved, bf16[16,2,16,128]{3,2,1,0:T(8,128)(2,1)S(1)} %get-tuple-element.10.rows, bf16[16,4,128]{2,1,0:T(4,128)(2,1)S(1)} %get-tuple-element.11.newest), custom_call_target="tpu_custom_call" | custom-call | tf_op jit(solution)/shard_map/pallas_call | solution.py:411

commit v5 on v4

--- a/solution.py
+++ b/solution.py
@@ -14,7 +14,7 @@
 BATCH = 32
 SLOTS = 256
 GROUPS = 16
-CUTS = (96, 96, 64)
+CUTS = (128, 80, 48)
 CHUNKS = len(CUTS)
 F32 = jnp.float32
 BF16 = jnp.bfloat16
@@ -35,13 +35,13 @@
 
 def kernel(
     matching, lengths, queries_in, kv, fresh_in, residual_in, weight, gain_in,
-    cache_out, rows_out, new_out,
+    cache_out, rows_out,
     queries, fresh, residual, gain,
     cache, fresh32, asked, attended, wide, partial, y_got, z_part, z_got, stream32, squares, sq_got,
-    mine, rows_got, rows_next, new_mine, new_got, new_next, got, nxt,
+    mine, rows_got, rows_next, got, nxt,
     small_sem, load_sem, weight_sem, send1, recv1, send2, recv2, own_sem,
     y_send, y_recv, z_send, z_recv, sq_send, sq_recv,
-    rs1, rr1, rs2, rr2, ns1, nr1, ns2, nr2,
+    rs1, rr1, rs2, rr2,
 ):
     me = lax.axis_index("section")
     zlo, x, core = me // 8, (me // 2) % 4, me % 2
@@ -106,16 +106,6 @@
     for copy in small:
         copy.wait()
     fresh32[...] = fresh[...].astype(F32)
-    for j in range(GROUPS):
-        pair = fresh32[2 * j : 2 * j + 2, :]
-        new_mine[j] = jnp.concatenate([pair[:, :HEAD], pair[:, HEAD:]], axis=0).astype(BF16)
-    new_copies = [
-        to(new_mine.at[p], new_got.at[me], ns1.at[k], nr1.at[k], section=p)
-        for k, p in enumerate(partners)
-    ]
-    for copy in new_copies:
-        copy.start()
-    new_got[me] = new_mine[me]
     for n in range(8):
         load_weight(n).start()
     for q in range(1, 2):
@@ -247,29 +237,14 @@
         stream = stream32[...].astype(BF16)
         for j in range(GROUPS):
             r, c = (j // 8) * 16, (j % 8) * HEAD
-            mine[j, 0] = stream[r : r + 16, c : c + HEAD]
-            mine[j, 1] = normed[r : r + 16, c : c + HEAD]
+            mine[j, 0:16] = stream[r : r + 16, c : c + HEAD]
+            mine[j, 16:32] = normed[r : r + 16, c : c + HEAD]
+            pair = fresh32[2 * j : 2 * j + 2, :]
+            both = jnp.concatenate([pair[:, :HEAD], pair[:, HEAD:]], axis=0)
+            mine[j, 32:36] = both.astype(BF16)
         for copy in row_copies:
             copy.start()
         rows_got[me] = mine[me]
-
-    new_copies2 = [
-        to(new_next.at[p], new_out.at[me], ns2.at[k], nr2.at[k], section=p)
-        for k, p in enumerate(partners)
-    ]
-
-    def turn_new():
-        for copy in new_copies:
-            copy.wait_recv()
-
-        def pick_new(p, _):
-            new_next[p] = new_got[matching[p]]
-            return 0
-
-        lax.fori_loop(0, GROUPS, pick_new, 0)
-        for copy in new_copies2:
-            copy.start()
-        new_out[me] = new_next[me]
 
     def turn_rows():
         for copy in row_copies:
@@ -286,7 +261,6 @@
 
     sum_y()
     spread_all(2)
-    turn_new()
     sum_z()
     turn(0)
     norm()
@@ -298,7 +272,7 @@
         for z2 in range(2):
             y_part(i, z2).wait_send()
     z_copy.wait_send()
-    for copy in sq_copies + row_copies + new_copies:
+    for copy in sq_copies + row_copies:
         copy.wait_send()
     for q in range(CHUNKS):
         for k in range(PARTNERS):
@@ -307,7 +281,7 @@
         for copy in pass_on(q):
             copy.wait()
         leave(q).wait()
-    for copy in row_copies2 + new_copies2:
+    for copy in row_copies2:
         copy.wait()
 
 
@@ -315,13 +289,13 @@
 
 
 def finish(
-    lengths, moved, rows, newest, cache_out, stream_out, normed_out,
+    lengths, moved, rows, cache_out, stream_out, normed_out,
     cache, stream, normed, sems, row_sems,
 ):
     for j in range(GROUPS):
         r, c = (j // 8) * 16, (j % 8) * HEAD
-        stream[r : r + 16, c : c + HEAD] = rows[j, 0]
-        normed[r : r + 16, c : c + HEAD] = rows[j, 1]
+        stream[r : r + 16, c : c + HEAD] = rows[j, 0:16]
+        normed[r : r + 16, c : c + HEAD] = rows[j, 16:32]
     row_copies = [
         pltpu.make_async_copy(stream, stream_out, row_sems.at[0]),
         pltpu.make_async_copy(normed, normed_out, row_sems.at[1]),
@@ -337,7 +311,7 @@
 
     def write(i, _):
         for b in range(STEP):
-            new = newest[i * (STEP // 2) + b // 2].astype(F32)
+            new = rows[i * (STEP // 2) + b // 2, 32:36].astype(F32)
             here = place == lengths[i * STEP + b].astype(F32).astype(BF16)
             for half in range(2):
                 row = 2 * half + b % 2
@@ -363,18 +337,16 @@
     anywhere = pl.BlockSpec(memory_space=pl.ANY)
     hbm = pl.BlockSpec(memory_space=pltpu.HBM)
     chunks = [pltpu.VMEM((GROUPS, 2, cut, 2 * HEAD), BF16) for cut in CUTS]
-    rows = pltpu.VMEM((GROUPS, 2, 16, HEAD), BF16)
-    new = pltpu.VMEM((GROUPS, 4, HEAD), BF16)
+    rows = pltpu.VMEM((GROUPS, 36, HEAD), BF16)
     dma = pltpu.SemaphoreType.DMA
-    moved, rows_moved, new_moved = pl.pallas_call(
+    moved, rows_moved = pl.pallas_call(
         kernel,
         out_shape=(
             jax.ShapeDtypeStruct((BATCH, SLOTS, 2 * HEAD), BF16),
-            jax.ShapeDtypeStruct((GROUPS, 2, 16, HEAD), BF16),
-            jax.ShapeDtypeStruct((GROUPS, 4, HEAD), BF16),
+            jax.ShapeDtypeStruct((GROUPS, 36, HEAD), BF16),
         ),
         in_specs=[smem, smem] + [hbm] * 6,
-        out_specs=(anywhere, vmem, vmem),
+        out_specs=(anywhere, vmem),
         scratch_shapes=[
             pltpu.VMEM((BATCH, 1024), BF16),
             pltpu.VMEM((BATCH, 2 * HEAD), BF16),
@@ -392,14 +364,14 @@
             pltpu.VMEM((BATCH, 1024), F32),
             pltpu.VMEM((8, HEAD), F32),
             pltpu.VMEM((7, 8, HEAD), F32),
-            rows, rows, rows, new, new, new,
+            rows, rows, rows,
             chunks, chunks,
             dma((4,)), dma, dma((8,)),
             dma((CHUNKS, PARTNERS)), dma((CHUNKS, PARTNERS)),
             dma((CHUNKS, PARTNERS)), dma((CHUNKS, PARTNERS)),
             dma((2, CHUNKS)),
             dma((3, 2)), dma((3, 2)), dma, dma, dma((7,)), dma((7,)),
-            *([dma((PARTNERS,))] * 8),
+            *([dma((PARTNERS,))] * 4),
         ],
         compiler_params=pltpu.CompilerParams(
             collective_id=0, has_side_effects=True, vmem_limit_bytes=34 << 20
@@ -415,7 +387,7 @@
             jax.ShapeDtypeStruct((BATCH, 1024), BF16),
             jax.ShapeDtypeStruct((BATCH, 1024), BF16),
         ),
-        in_specs=[smem, vmem, vmem, vmem],
+        in_specs=[smem, vmem, vmem],
         out_specs=(hbm, hbm, hbm),
         scratch_shapes=[
             pltpu.VMEM((BATCH, SLOTS, 2 * HEAD), BF16),
@@ -425,7 +397,7 @@
             dma((2,)),
         ],
         compiler_params=pltpu.CompilerParams(vmem_limit_bytes=12 << 20),
-    )(stay(lengths), moved, rows_moved, new_moved)
+    )(stay(lengths), moved, rows_moved)
     return cache_out[None], stream_out[None], normed_out[None]
 
 

time: 112 us -> 112 us (level)
  no operation moved by 1% of the time
where the time goes in v5:
time: 112 us
  Pallas kernels  111 us (99%)
    pallas_call x1, Pallas kernels, on_device(): pl.pallas_call(kernel, out_shape=(jax.ShapeDtypeStruct((BATCH, SLOTS, 2 *...  108 us
    pallas_call x1, Pallas kernels, on_device(): pl.pallas_call(finish, out_shape=(jax.ShapeDtypeStruct((BATCH, SLOTS, 2 *...  2.9 us

profile of v5, /device:TPU:1, one launch (start us, length us, event | category | flops | bytes accessed | tf_op | source)
XLA Modules:
  0.0 111.7 jit_solution(12148280384892801632)
XLA Ops:
  0.6 108.2 %shard_map.103 = (bf16[32,256,256]{2,1,0:T(8,128)(2,1)S(1)}, bf16[16,36,128]{2,1,0:T(8,128)(2,1)S(1)}) custom-call(s32[16]{0:T(128)} %matching.1, s32[32]{0:T(128)} %lengths.3, bf16[32,1024]{1,0:T(8,128)(2,1)} %bitcast.10, bf16[32,256,256]{2,1,0:T(8,128)(2,1)} %bitcast.9, bf16[32,256]{1,0:T(8,128)(2,1)} %bitcast.12, bf16[32,1024]{1,0:T(8,128)(2,1)} %bitcast.11, ...), custom_call_target="tpu_custom_call" | custom-call | tf_op jit(solution)/shard_map/pallas_call | solution.py:342
  108.8 2.9 %shard_map.104 = (bf16[32,256,256]{2,1,0:T(8,128)(2,1)}, bf16[32,1024]{1,0:T(8,128)(2,1)}, bf16[32,1024]{1,0:T(8,128)(2,1)}) custom-call(s32[32]{0:T(128)} %lengths.3, bf16[32,256,256]{2,1,0:T(8,128)(2,1)S(1)} %get-tuple-element.8.moved, bf16[16,36,128]{2,1,0:T(8,128)(2,1)S(1)} %get-tuple-element.9.rows), custom_call_target="tpu_custom_call" | custom-call | tf_op jit(solution)/shard_map/pallas_call | solution.py:383

commit v6 on v5

--- a/solution.py
+++ b/solution.py
@@ -182,7 +182,7 @@
             return 0
 
         lax.fori_loop(0, GROUPS, pick, 0)
-        for copy in pass_on(q):
+        for copy in pass_on(q)[::-1]:
             copy.start()
         leave(q).start()
 

time: 112 us -> 112 us (level)
  no operation moved by 1% of the time
where the time goes in v6:
time: 112 us; the launch traced here: 111 us
  Pallas kernels  110 us (98%)
    pallas_call x1, Pallas kernels, on_device(): pl.pallas_call(kernel, out_shape=(jax.ShapeDtypeStruct((BATCH, SLOTS, 2 *...  108 us
    pallas_call x1, Pallas kernels, on_device(): pl.pallas_call(finish, out_shape=(jax.ShapeDtypeStruct((BATCH, SLOTS, 2 *...  2.9 us

profile of v6, /device:TPU:1, one launch (start us, length us, event | category | flops | bytes accessed | tf_op | source)
XLA Modules:
  0.0 111.1 jit_solution(15645401607002063346)
XLA Ops:
  0.6 107.5 %shard_map.103 = (bf16[32,256,256]{2,1,0:T(8,128)(2,1)S(1)}, bf16[16,36,128]{2,1,0:T(8,128)(2,1)S(1)}) custom-call(s32[16]{0:T(128)} %matching.1, s32[32]{0:T(128)} %lengths.3, bf16[32,1024]{1,0:T(8,128)(2,1)} %bitcast.10, bf16[32,256,256]{2,1,0:T(8,128)(2,1)} %bitcast.9, bf16[32,256]{1,0:T(8,128)(2,1)} %bitcast.12, bf16[32,1024]{1,0:T(8,128)(2,1)} %bitcast.11, ...), custom_call_target="tpu_custom_call" | custom-call | tf_op jit(solution)/shard_map/pallas_call | solution.py:342
  108.1 2.9 %shard_map.104 = (bf16[32,256,256]{2,1,0:T(8,128)(2,1)}, bf16[32,1024]{1,0:T(8,128)(2,1)}, bf16[32,1024]{1,0:T(8,128)(2,1)}) custom-call(s32[32]{0:T(128)} %lengths.3, bf16[32,256,256]{2,1,0:T(8,128)(2,1)S(1)} %get-tuple-element.8.moved, bf16[16,36,128]{2,1,0:T(8,128)(2,1)S(1)} %get-tuple-element.9.rows), custom_call_target="tpu_custom_call" | custom-call | tf_op jit(solution)/shard_map/pallas_call | solution.py:383
